TPU v7x, 32 devices: a whole 2x2x4 slice. The times are simulated.
32 devices in a mesh: gx: 4 (over z), gy: 4 (over x, core), gz: 2 (over y).
Axes of the slice: x: 2, y: 2, z: 4, core: 2. Of those that a mesh axis runs over, the one named last changes fastest.
Arguments:
- moving_image: float32 [64, 128, 512], P('gz', 'gx', 'gy'), may hold values from -6 to 6
- fixed_image: float32 [64, 128, 512], P('gz', 'gx', 'gy'), may hold values from -6 to 6
- subvoxel: float32 [3], replicated, may hold values from 0.05 to 0.95
- brick_offset: int32 [2, 8, 32], P(None, 'gx', 'gy'), may hold values from -16 to 16, as said below
Outputs:
- brick_ncc: float32 [8, 32], P('gx', 'gy')
- control_grad: float32 [3, 4, 8, 32], P(None, None, 'gx', 'gy')
Inputs may be any that keep to these rules, and one draw needn't show every extreme that they name: `brick_offset`: row 0 of each draw holds both -16 and 16 somewhere, and so does row 1.
All inputs are finite; a program needn't handle non-finite values.
Results may differ from a plain program's by a relative error of at most 0.00023.
Values sent between devices are 32-bit elements; how exact they have to be, the bound alone decides.
A program may use at most 128 MiB of HBM per device.

v0:
```python
import math

import jax
import jax.numpy as jnp
from jax import lax
from jax.sharding import PartitionSpec as P

NZ = 64
BRICK = 16
RANGE = 16


EPSILON = 1e-06
SUPPORT_NORM = 64.0


def with_halo(array, sides, width):
    for axis, dim in sides:
        size, length = (lax.axis_size(axis), array.shape[dim])
        up = [(i, (i + 1) % size) for i in range(size - 1)]
        down = [(j, i) for i, j in up]
        last = lax.slice_in_dim(array, length - width, length, axis=dim)
        leading = lax.slice_in_dim(array, 0, width, axis=dim)
        before = lax.ppermute(last, axis, up)
        after = lax.ppermute(leading, axis, down)
        array = jnp.concatenate([before, array, after], axis=dim)
    return array


def inverse_rows(row_first, row_count, col_first, col_count, line_len):
    row_pos = row_first + jnp.arange(row_count, dtype=jnp.int32) + 1
    col_pos = col_first + jnp.arange(col_count, dtype=jnp.int32) + 1
    nearer = jnp.minimum(row_pos[:, None], col_pos[None, :])
    farther = jnp.maximum(row_pos[:, None], col_pos[None, :])
    log_pole = math.log(2.0 + math.sqrt(3.0))
    nearer_f = nearer.astype(jnp.float32)
    farther_f = farther.astype(jnp.float32)
    entry = jnp.exp((nearer_f - farther_f) * log_pole) * (1.0 - jnp.exp(-2.0 * log_pole * nearer_f))
    entry = entry * (1.0 - jnp.exp(-2.0 * log_pole * (line_len + 1 - farther_f)))
    entry = entry / (
        (math.exp(log_pole) - math.exp(-log_pole))
        * (1.0 - math.exp(-2.0 * log_pole * (line_len + 1)))
    )
    parity = 1.0 - 2.0 * ((nearer + farther) % 2).astype(jnp.float32)
    row_inside = (row_pos >= 1) & (row_pos <= line_len)
    col_inside = (col_pos >= 1) & (col_pos <= line_len)
    inside = row_inside[:, None] & col_inside[None, :]
    return jnp.where(inside, 6.0 * parity * entry, 0.0)


def tap_weights(subvoxel):
    smooth = jnp.stack(
        [
            (1.0 - subvoxel) ** 3 / 6.0,
            (3.0 * subvoxel**3 - 6.0 * subvoxel**2 + 4.0) / 6.0,
            (-3.0 * subvoxel**3 + 3.0 * subvoxel**2 + 3.0 * subvoxel + 1.0) / 6.0,
            subvoxel**3 / 6.0,
        ]
    )
    slope = jnp.stack(
        [
            -((1.0 - subvoxel) ** 2) / 2.0,
            (3.0 * subvoxel**2 - 4.0 * subvoxel) / 2.0,
            (-3.0 * subvoxel**2 + 2.0 * subvoxel + 1.0) / 2.0,
            subvoxel**2 / 2.0,
        ]
    )
    return (smooth, slope)


def apply_taps(volume, along, weights):
    span_len = volume.shape[along] - 3
    running = weights[0] * lax.slice_in_dim(volume, 0, span_len, axis=along)
    for tap_num in range(1, 4):
        running = running + weights[tap_num] * lax.slice_in_dim(
            volume, tap_num, tap_num + span_len, axis=along
        )
    return running


def spread(depth_pair, smooth_x, slope_x, smooth_y, slope_y):
    x_smooth = apply_taps(depth_pair, 2, smooth_x)
    x_slope = apply_taps(depth_pair[0], 1, slope_x)
    value_field = apply_taps(x_smooth[0], 2, smooth_y)
    slope_dz = apply_taps(x_smooth[1], 2, smooth_y)
    slope_dx = apply_taps(x_slope, 2, smooth_y)
    slope_dy = apply_taps(x_smooth[0], 2, slope_y)
    return jnp.stack([value_field, slope_dx, slope_dy, slope_dz])


def resample(fields, brick_offset):
    span_x = fields.shape[2] - 2 * RANGE
    span_y = fields.shape[3] - 2 * RANGE
    shift_x = jnp.repeat(jnp.repeat(brick_offset[0], BRICK, axis=0), BRICK, axis=1)
    shift_y = jnp.repeat(jnp.repeat(brick_offset[1], BRICK, axis=0), BRICK, axis=1)
    source_x = jnp.arange(span_x, dtype=jnp.int32)[:, None] + shift_x + RANGE
    source_y = jnp.arange(span_y, dtype=jnp.int32)[None, :] + shift_y + RANGE
    return fields[:, :, source_x, source_y]


def brick_sums(volume):
    depth_len, width_x, width_y = volume.shape
    return volume.reshape(depth_len, width_x // BRICK, BRICK, width_y // BRICK, BRICK).sum(
        axis=(0, 2, 4)
    )


def expand(per_brick):
    return jnp.repeat(jnp.repeat(per_brick, BRICK, axis=0), BRICK, axis=1)[None]


def bspline(offset):
    magnitude = jnp.abs(offset)
    inner = 2.0 / 3.0 - magnitude * magnitude + 0.5 * magnitude * magnitude * magnitude
    outer = jnp.maximum(2.0 - magnitude, 0.0) ** 3 / 6.0
    return jnp.where(magnitude < 1.0, inner, outer)


def basis(point_count, first_point, cell_count, first_cell):
    points = first_point + jnp.arange(point_count, dtype=jnp.int32)
    cell_pos = first_cell + jnp.arange(cell_count, dtype=jnp.int32)
    offset = (cell_pos[None, :] - BRICK * points[:, None] - BRICK // 2).astype(jnp.float32) / BRICK
    return bspline(offset)


def shards(moving_image, fixed_image, subvoxel, brick_offset):
    depth_len, width_x, width_y = moving_image.shape
    start_x = lax.axis_index("gx") * width_x
    start_y = lax.axis_index("gy") * width_y
    start_z = lax.axis_index("gz") * depth_len
    total_x = width_x * lax.axis_size("gx")
    total_y = width_y * lax.axis_size("gy")
    margin = 12
    widened = with_halo(moving_image, (("gx", 1),), margin)
    matrix_x = inverse_rows(start_x, width_x, start_x - margin, width_x + 2 * margin, total_x)
    along_x = jnp.einsum("ab,zbc->zac", matrix_x, widened, precision=lax.Precision.HIGHEST)
    widened = with_halo(along_x, (("gy", 2),), margin)
    matrix_y = inverse_rows(start_y - margin, width_y + 2 * margin, start_y, width_y, total_y)
    along_y = jnp.dot(
        widened.reshape(-1, width_y + 2 * margin), matrix_y, precision=lax.Precision.HIGHEST
    )
    along_y = along_y.reshape(depth_len, width_x, width_y)
    widened = with_halo(along_y, (("gz", 0),), margin)
    matrix_z = inverse_rows(start_z, depth_len, start_z - margin, depth_len + 2 * margin, NZ)
    coeffs = jnp.einsum("ab,bxy->axy", matrix_z, widened, precision=lax.Precision.HIGHEST)
    smooth_w, slope_w = tap_weights(subvoxel)
    depth_ext = with_halo(coeffs, (("gz", 0),), 2)
    depth_ext = depth_ext[1:]
    depth_pair = jnp.stack(
        [apply_taps(depth_ext, 0, smooth_w[:, 0]), apply_taps(depth_ext, 0, slope_w[:, 0])]
    )
    reach_cells = RANGE + 2
    widened = with_halo(depth_pair, (("gx", 2), ("gy", 3)), reach_cells)
    fields = spread(
        widened[:, :, 1:, 1:], smooth_w[:, 1], slope_w[:, 1], smooth_w[:, 2], slope_w[:, 2]
    )
    global_x = start_x - RANGE + jnp.arange(width_x + 2 * RANGE, dtype=jnp.int32)
    global_y = start_y - RANGE + jnp.arange(width_y + 2 * RANGE, dtype=jnp.int32)
    inside_x = (global_x >= 0) & (global_x < total_x)
    inside_y = (global_y >= 0) & (global_y < total_y)
    inside = inside_x[:, None] & inside_y[None, :]
    fields = jnp.where(inside[None, None], fields, 0.0)
    picked = resample(fields, brick_offset)
    warped = picked[0]
    voxel_count = NZ * BRICK * BRICK
    sum_fixed, sum_warped = lax.psum((brick_sums(fixed_image), brick_sums(warped)), "gz")
    centered_f = fixed_image - expand(sum_fixed / voxel_count)
    centered_w = warped - expand(sum_warped / voxel_count)
    fixed_sq, warped_sq, cross_sum = lax.psum(
        (
            brick_sums(centered_f * centered_f),
            brick_sums(centered_w * centered_w),
            brick_sums(centered_f * centered_w),
        ),
        "gz",
    )
    inv_norm = lax.rsqrt(fixed_sq * warped_sq + EPSILON)
    brick_ncc = cross_sum * inv_norm
    slope_ratio = cross_sum / (warped_sq + EPSILON)
    gradient = voxel_count * expand(inv_norm) * (centered_f - expand(slope_ratio) * centered_w)
    forces = gradient[None] * picked[1:4]
    basis_x = basis(width_x // BRICK + 4, start_x // BRICK - 2, width_x, start_x)
    basis_y = basis(width_y // BRICK + 4, start_y // BRICK - 2, width_y, start_y)
    basis_z = basis(NZ // BRICK, 0, depth_len, start_z)
    partial_y = jnp.einsum("dzxy,jy->dzxj", forces, basis_y, precision=lax.Precision.HIGHEST)
    partial_x = jnp.einsum("dzxj,ix->dzij", partial_y, basis_x, precision=lax.Precision.HIGHEST)
    partial_z = (
        jnp.einsum("dzij,kz->dkij", partial_x, basis_z, precision=lax.Precision.HIGHEST)
        / SUPPORT_NORM
    )
    summed = lax.psum(partial_z, "gz")
    ext_x = summed.shape[2]
    edges_x = jnp.concatenate([summed[:, :, :2], summed[:, :, ext_x - 2 :]], axis=2)
    from_x = with_halo(edges_x, (("gx", 2),), 2)
    inner_x = summed[:, :, 2 : ext_x - 2]
    inner_x = inner_x.at[:, :, :2].add(from_x[:, :, :2])
    inner_x = inner_x.at[:, :, ext_x - 6 :].add(from_x[:, :, 6:])
    ext_y = inner_x.shape[3]
    edges_y = jnp.concatenate([inner_x[:, :, :, :2], inner_x[:, :, :, ext_y - 2 :]], axis=3)
    from_y = with_halo(edges_y, (("gy", 3),), 2)
    control_grad = inner_x[:, :, :, 2 : ext_y - 2]
    control_grad = control_grad.at[:, :, :, :2].add(from_y[:, :, :, :2])
    control_grad = control_grad.at[:, :, :, ext_y - 6 :].add(from_y[:, :, :, 6:])
    return (brick_ncc, control_grad)


def solution(mesh):
    return jax.shard_map(
        shards,
        mesh=mesh,
        in_specs=(P("gz", "gx", "gy"), P("gz", "gx", "gy"), P(), P(None, "gx", "gy")),
        out_specs=(P("gx", "gy"), P(None, None, "gx", "gy")),
        check_vma=False,
    )
```

profile of v0, /device:TPU:1, one launch (start us, length us, event | category | flops | bytes accessed | tf_op | source)
XLA Modules:
  0.0 251.0 jit_solution(4143564535132998514)
XLA Ops:
  0.6 1.1 fusion.313
  1.7 4.0 %collective-permute-start = (f32[32,12,128]{2,1,0:T(8,128)S(1)}, f32[32,12,128]{2,1,0:T(8,128)S(1)}, u32[]{:S(2)}, u32[]{:S(2)}) collective-permute-start(f32[32,12,128]{2,1,0:T(8,128)S(1)} %get-tuple-element.95), channel_id=1, source_target_pairs={{0,8},{8,16},{16,24},{1,9},{9,17},{17,25},{2,10},{10,18},{18,26},{... | collective-permute-start | bytes 589832 | tf_op jit(solution)/shard_map/ppermute | solution.py:24
  5.8 1.3 collective-permute-start.1
  7.2 0.7 fusion.246
  7.9 0.7 fusion.316
  8.5 0.7 fusion.318
  9.2 0.7 fusion.320
  9.9 0.7 fusion.322
  10.7 3.8 %collective-permute-done.1 = f32[32,12,128]{2,1,0:T(8,128)S(1)} collective-permute-done((f32[32,12,128]{2,1,0:T(8,128)S(1)}, f32[32,12,128]{2,1,0:T(8,128)S(1)}, u32[]{:S(2)}, u32[]{:S(2)}) %collective-permute-start.1) | collective-permute-done | bytes 196640 | tf_op jit(solution)/shard_map/ppermute | solution.py:25
  14.6 1.8 convolution_bitcast_fusion
  16.6 4.8 %collective-permute-start.2 = (f32[32,32,12]{2,1,0:T(8,128)S(1)}, f32[32,32,12]{2,1,0:T(8,128)S(1)}, u32[]{:S(2)}, u32[]{:S(2)}) collective-permute-start(f32[32,32,12]{2,1,0:T(8,128)S(1)} %get-tuple-element.93), channel_id=1, source_target_pairs={{0,2},{2,4},{4,6},{1,3},{3,5},{5,7},{8,10},{10,12},{12,14},{9,11},... | collective-permute-start | bytes 147464 | tf_op jit(solution)/shard_map/ppermute | solution.py:24
  21.4 1.9 collective-permute-start.3
  23.4 4.2 %collective-permute-done.2 = f32[32,32,12]{2,1,0:T(8,128)S(1)} collective-permute-done((f32[32,32,12]{2,1,0:T(8,128)S(1)}, f32[32,32,12]{2,1,0:T(8,128)S(1)}, u32[]{:S(2)}, u32[]{:S(2)}) %collective-permute-start.2) | collective-permute-done | bytes 49184 | tf_op jit(solution)/shard_map/ppermute | solution.py:24
  27.5 4.4 %collective-permute-done.3 = f32[32,32,12]{2,1,0:T(8,128)S(1)} collective-permute-done((f32[32,32,12]{2,1,0:T(8,128)S(1)}, f32[32,32,12]{2,1,0:T(8,128)S(1)}, u32[]{:S(2)}, u32[]{:S(2)}) %collective-permute-start.3) | collective-permute-done | bytes 49184 | tf_op jit(solution)/shard_map/ppermute | solution.py:25
  32.4 1.1 fusion.43
  33.7 3.4 %collective-permute-start.4 = (f32[12,32,128]{2,0,1:T(8,128)S(1)}, f32[12,32,128]{2,0,1:T(8,128)S(1)}, u32[]{:S(2)}, u32[]{:S(2)}) collective-permute-start(f32[12,32,128]{2,0,1:T(8,128)S(1)} %copy.50), channel_id=1, source_target_pairs={{0,1},{2,3},{4,5},{6,7},{8,9},{10,11},{12,13},{14,15},{16,17},{18,... | collective-permute-start | bytes 589832 | tf_op jit(solution)/shard_map/ppermute | solution.py:24
  37.3 1.3 collective-permute-start.5
  39.0 1.5 collective-permute-done.4
  40.5 4.0 %collective-permute-done.5 = f32[12,32,128]{2,0,1:T(8,128)S(1)} collective-permute-done((f32[12,32,128]{2,0,1:T(8,128)S(1)}, f32[12,32,128]{2,0,1:T(8,128)S(1)}, u32[]{:S(2)}, u32[]{:S(2)}) %collective-permute-start.5) | collective-permute-done | bytes 196640 | tf_op jit(solution)/shard_map/ppermute | solution.py:25
  44.4 0.7 fusion.21
  45.2 1.5 collective-permute-start.6
  46.7 1.3 collective-permute-start.7
  48.0 3.3 %collective-permute-done.7 = f32[2,32,128]{2,0,1:T(2,128)S(1)} collective-permute-done((f32[2,32,128]{2,0,1:T(2,128)S(1)}, f32[2,32,128]{2,0,1:T(2,128)S(1)}, u32[]{:S(2)}, u32[]{:S(2)}) %collective-permute-start.7) | collective-permute-done | bytes 32800 | tf_op jit(solution)/shard_map/ppermute | solution.py:25
  51.3 2.7 %add_bitcast_fusion.2 = f32[1,32,32,128]{3,1,2,0:T(8,128)S(1)} fusion(f32[32,32,128]{2,0,1:T(8,128)S(1)} %fusion.21, f32[2,32,128]{2,0,1:T(2,128)S(1)} %collective-permute-done.6, f32[2,32,128]{2,0,1:T(2,128)S(1)} %collective-permute-done.7, f32[]{:T(128)} %bitcast.26, f32[]{:T(128)} %bitcast.24, f32[]{:T(128)} %bitcast.22, f32[]{:T(128)} %bitcast.20), kind=kLoop, calls=%fused_computation.73 | loop fusion | flops 1310720 | bytes 1114128 | tf_op jit(solution)/shard_map/stack | solution.py:149
  54.1 2.8 %add_bitcast_fusion.3 = f32[1,32,32,128]{3,1,2,0:T(8,128)S(1)} fusion(f32[32,32,128]{2,0,1:T(8,128)S(1)} %fusion.21, f32[2,32,128]{2,0,1:T(2,128)S(1)} %collective-permute-done.6, f32[2,32,128]{2,0,1:T(2,128)S(1)} %collective-permute-done.7, f32[]{:T(128)} %bitcast.17, f32[]{:T(128)} %bitcast.15, f32[]{:T(128)} %bitcast.13, f32[]{:T(128)} %bitcast.4), kind=kLoop, calls=%fused_computation.74 | loop fusion | flops 1310720 | bytes 1114128 | tf_op jit(solution)/shard_map/stack | solution.py:149
  56.9 1.1 fusion.28
  58.1 3.2 %collective-permute-start.8 = (f32[2,32,18,128]{3,1,2,0:T(8,128)}, f32[2,32,18,128]{3,1,2,0:T(8,128)S(1)}, u32[]{:S(2)}, u32[]{:S(2)}) collective-permute-start(f32[2,32,18,128]{3,1,2,0:T(8,128)} %get-tuple-element.87), channel_id=1, source_target_pairs={{0,8},{8,16},{16,24},{1,9},{9,17},{17,25},{2,10},{10,18},{18,26},{... | collective-permute-start | bytes 1769480 | tf_op jit(solution)/shard_map/ppermute | solution.py:24
  61.3 1.3 collective-permute-start.9
  63.5 7.2 %collective-permute-done.8 = f32[2,32,18,128]{3,1,2,0:T(8,128)S(1)} collective-permute-done((f32[2,32,18,128]{3,1,2,0:T(8,128)}, f32[2,32,18,128]{3,1,2,0:T(8,128)S(1)}, u32[]{:S(2)}, u32[]{:S(2)}) %collective-permute-start.8) | collective-permute-done | bytes 589856 | tf_op jit(solution)/shard_map/ppermute | solution.py:24
  70.7 4.0 %collective-permute-done.9 = f32[2,32,18,128]{3,1,2,0:T(8,128)S(1)} collective-permute-done((f32[2,32,18,128]{3,1,2,0:T(8,128)}, f32[2,32,18,128]{3,1,2,0:T(8,128)S(1)}, u32[]{:S(2)}, u32[]{:S(2)}) %collective-permute-start.9) | collective-permute-done | bytes 589856 | tf_op jit(solution)/shard_map/ppermute | solution.py:25
  74.8 0.8 copy-done.3
  75.8 2.2 fusion.309
  77.9 3.8 %copy.53 = f32[2,32,68,18]{2,1,3,0:T(8,128)} copy(f32[2,32,68,18]{3,1,2,0:T(8,128)} %get-tuple-element.83) | data formatting | bytes 626688 | tf_op jit(solution)/shard_map/slice | solution.py:22
  81.7 3.1 %collective-permute-start.10 = (f32[2,32,68,18]{2,1,3,0:T(8,128)}, f32[2,32,68,18]{2,1,3,0:T(8,128)}, u32[]{:S(2)}, u32[]{:S(2)}) collective-permute-start(f32[2,32,68,18]{2,1,3,0:T(8,128)} %copy.53), channel_id=1, source_target_pairs={{0,2},{2,4},{4,6},{1,3},{3,5},{5,7},{8,10},{10,12},{12,14},{9,11},... | collective-permute-start | bytes 940040 | tf_op jit(solution)/shard_map/ppermute | solution.py:24
  84.9 2.3 copy.54
  87.2 2.1 collective-permute-start.11
  89.4 2.5 %collective-permute-done.10 = f32[2,32,68,18]{2,1,3,0:T(8,128)} collective-permute-done((f32[2,32,68,18]{2,1,3,0:T(8,128)}, f32[2,32,68,18]{2,1,3,0:T(8,128)}, u32[]{:S(2)}, u32[]{:S(2)}) %collective-permute-start.10) | collective-permute-done | bytes 313376 | tf_op jit(solution)/shard_map/ppermute | solution.py:24
  92.0 3.1 %copy.55 = f32[2,32,68,18]{3,1,2,0:T(8,128)S(1)} copy(f32[2,32,68,18]{2,1,3,0:T(8,128)} %collective-permute-done.10) | data formatting | bytes 626688 | tf_op jit(solution)/shard_map/ppermute | solution.py:24
  95.1 3.6 %collective-permute-done.11 = f32[2,32,68,18]{2,1,3,0:T(8,128)} collective-permute-done((f32[2,32,68,18]{2,1,3,0:T(8,128)}, f32[2,32,68,18]{2,1,3,0:T(8,128)}, u32[]{:S(2)}, u32[]{:S(2)}) %collective-permute-start.11) | collective-permute-done | bytes 313376 | tf_op jit(solution)/shard_map/ppermute | solution.py:25
  98.7 4.1 %copy.56 = f32[2,32,68,18]{3,1,2,0:T(8,128)} copy(f32[2,32,68,18]{2,1,3,0:T(8,128)} %collective-permute-done.11) | data formatting | bytes 626688 | tf_op jit(solution)/shard_map/ppermute | solution.py:25
  102.8 4.4 %pad_maximum_fusion = f32[2,32,68,164]{3,1,2,0:T(8,128)S(1)} fusion(f32[2,32,68,18]{3,1,2,0:T(8,128)} %copy.56, f32[2,32,18,128]{3,1,2,0:T(8,128)} %copy-done.3, f32[1,32,32,128]{3,1,2,0:T(8,128)S(1)} %add_bitcast_fusion.2, f32[1,32,32,128]{3,1,2,0:T(8,128)S(1)} %add_bitcast_fusion.3, f32[2,32,18,128]{3,1,2,0:T(8,128)} %copy-done.2, ...), kind=kLoop, calls=%fused_computation.2 | loop fusion | flops 3568640 | bytes 5709824 | tf_op jit(solution)/shard_map/concatenate | solution.py:26
  107.2 0.6 slice_bitcast_fusion
  107.8 7.1 %fusion = f32[2,32,64,163]{3,1,2,0:T(8,128)S(1)} fusion(f32[2,32,68,164]{3,1,2,0:T(8,128)S(1)} %pad_maximum_fusion, f32[]{:T(128)} %bitcast.30, f32[]{:T(128)} %bitcast.29, f32[]{:T(128)} %bitcast.28, f32[]{:T(128)} %bitcast.3), kind=kLoop, calls=%fused_computation.4 | loop fusion | flops 4673536 | bytes 13352976 | tf_op jit(solution)/shard_map/add | solution.py:75
  115.5 4.1 %fusion.4 = f32[1,32,64,160]{3,1,2,0:T(8,128)S(1)} fusion(f32[32,64,163]{2,0,1:T(8,128)S(1)} %get-tuple-element.82, f32[]{:T(128)} %bitcast.34, f32[]{:T(128)} %bitcast.33, f32[]{:T(128)} %bitcast.32, f32[]{:T(128)} %bitcast.2), kind=kLoop, calls=%fused_computation.14 | loop fusion | flops 2293760 | bytes 6553616 | tf_op jit(solution)/shard_map/stack | solution.py:88
  119.7 3.1 %fusion.11 = f32[32,64,163]{2,0,1:T(8,128)S(1)} fusion(f32[32,67,163]{2,0,1:T(8,128)S(1)} %slice_bitcast_fusion, f32[]{:T(128)} %bitcast.40, f32[]{:T(128)} %bitcast.39, f32[]{:T(128)} %bitcast.38, f32[]{:T(128)} %bitcast.36), kind=kLoop, calls=%fused_computation.30 | loop fusion | flops 2336768 | bytes 6676496 | tf_op jit(solution)/shard_map/add | solution.py:75
  122.8 4.1 %fusion.8 = f32[1,32,64,160]{3,1,2,0:T(8,128)S(1)} fusion(f32[32,64,163]{2,0,1:T(8,128)S(1)} %fusion.11, f32[]{:T(128)} %bitcast.34, f32[]{:T(128)} %bitcast.33, f32[]{:T(128)} %bitcast.32, f32[]{:T(128)} %bitcast.2), kind=kLoop, calls=%fused_computation.23 | loop fusion | flops 2293760 | bytes 6553616 | tf_op jit(solution)/shard_map/stack | solution.py:88
  126.9 6.5 %add_bitcast_fusion.1 = (f32[1,32,64,160]{3,1,2,0:T(8,128)S(1)}, f32[1,32,64,160]{3,1,2,0:T(8,128)S(1)}) fusion(f32[32,64,163]{2,0,1:T(8,128)S(1)} %get-tuple-element.81, f32[]{:T(128)} %bitcast.34, f32[]{:T(128)} %bitcast.33, f32[]{:T(128)} %bitcast.32, f32[]{:T(128)} %bitcast.2, f32[]{:T(128)} %bitcast.45, f32[]{:T(128)} %bitcast.44, f32[]{:T(128)} %bitcast.43, ...), kind=kLoop, calls=%fused_computation.38 | loop fusion | flops 4587520 | bytes 7864352 | tf_op jit(solution)/shard_map/stack | solution.py:88
  133.4 3.9 %maximum_select_fusion = f32[4,32,64,160]{3,1,2,0:T(8,128)} fusion(f32[1,32,64,160]{3,1,2,0:T(8,128)S(1)} %fusion.4, f32[1,32,64,160]{3,1,2,0:T(8,128)S(1)} %get-tuple-element.86, f32[1,32,64,160]{3,1,2,0:T(8,128)S(1)} %fusion.8, f32[1,32,64,160]{3,1,2,0:T(8,128)S(1)} %get-tuple-element.85, pred[64,160]{1,0:T(8,128)(4,1)S(1)} %broadcast_and_fusion), kind=kLoop, calls=%fused_computation.1 | loop fusion | flops 5242880 | bytes 10496000 | tf_op jit(solution)/shard_map/jit(_where)/select_n | solution.py:162
  137.3 16.9 %copy.60 = f32[4,32,64,160]{1,0,3,2:T(4,128)} copy(f32[4,32,64,160]{3,1,2,0:T(8,128)} %maximum_select_fusion) | data formatting | bytes 10485760 | tf_op jit(solution)/shard_map/jit(_where)/select_n | solution.py:162
  154.2 43.9 %gather_fusion = f32[4096,4,32]{2,1,0:T(4,128)} fusion(f32[4,32,64,160]{1,0,3,2:T(4,128)} %copy.60, s32[4096]{0:T(1024)S(1)} %bitcast.127), kind=kCustom, calls=%fused_computation | custom fusion | bytes 4227072 | tf_op jit(solution)/shard_map/gather | solution.py:98
  198.1 5.2 %copy.61 = f32[32,128,4,32]{1,0,3,2:T(8,128)S(1)} copy(f32[32,128,4,32]{3,2,1,0:T(4,128)} %bitcast.133) | data formatting | bytes 4194304 | tf_op jit(solution)/shard_map/gather | solution.py:98
  203.6 4.0 %all-reduce.1 = (f32[2,8]{1,0:T(2,128)S(1)}, f32[2,8]{1,0:T(2,128)S(1)}) all-reduce(f32[2,8]{1,0:T(2,128)S(1)} %reduce_sum.61, f32[2,8]{1,0:T(2,128)S(1)} %reduce_sum.67), channel_id=1, replica_groups=mesh['gx'=4,'gy'=4,'gz'=2] {'gz'}, use_global_device_ids=true, to_apply=%region_2.3 | all-reduce | flops 32 | bytes 256 | tf_op jit(solution)/shard_map/psum | solution.py:166
  209.1 3.8 %all-reduce = (f32[2,8]{1,0:T(2,128)S(1)}, f32[2,8]{1,0:T(2,128)S(1)}, f32[2,8]{1,0:T(2,128)S(1)}) all-reduce(f32[2,8]{1,0:T(2,128)S(1)} %reduce_sum.70, f32[2,8]{1,0:T(2,128)S(1)} %reduce_sum.91, f32[2,8]{1,0:T(2,128)S(1)} %reduce_sum.94), channel_id=1, replica_groups=mesh['gx'=4,'gy'=4,'gz'=2] {'gz'}, use_global_device_ids=true, to_apply=%region_8.9 | all-reduce | flops 48 | bytes 384 | tf_op jit(solution)/shard_map/psum | solution.py:169
  214.2 6.2 %fusion.14 = f32[3,32,32,12]{2,3,1,0:T(8,128)S(1)} fusion(f32[4,32,32,128]{3,2,1,0:T(8,128)S(1)} %bitcast.132, f32[32,32,128]{2,1,0:T(8,128)S(1)} %subtract_multiply_fusion, s32[12]{0:T(128)S(1)} %add_multiply_fusion, s32[128]{0:T(128)S(1)} %iota_add_fusion), kind=kOutput, calls=%fused_computation.40 | convolution fusion | flops 57043968 | bytes 2245632 | tf_op jit(solution)/shard_map/dzxy,jy->dzxj/dot_general | solution.py:185
  220.4 2.4 convolution_bitcast_fusion.1
  222.8 1.2 fusion.15
  224.0 5.4 %psum.47 = f32[3,4,6,12]{3,1,2,0:T(4,128)S(1)} all-reduce(f32[3,4,6,12]{3,1,2,0:T(4,128)S(1)} %fusion.15), channel_id=1, replica_groups=mesh['gx'=4,'gy'=4,'gz'=2] {'gz'}, use_global_device_ids=true, to_apply=%region_15.16 | all-reduce | flops 864 | bytes 6912 | tf_op jit(solution)/shard_map/psum | solution.py:191
  229.4 3.2 %collective-permute-start.12 = (f32[3,4,2,12]{3,1,2,0:T(4,128)S(1)}, f32[3,4,2,12]{3,1,2,0:T(4,128)S(1)}, u32[]{:S(2)}, u32[]{:S(2)}) collective-permute-start(f32[3,4,2,12]{3,1,2,0:T(4,128)S(1)} %get-tuple-element.97), channel_id=1, source_target_pairs={{0,8},{8,16},{16,24},{1,9},{9,17},{17,25},{2,10},{10,18},{18,26},{... | collective-permute-start | bytes 3464 | tf_op jit(solution)/shard_map/ppermute | solution.py:24
  232.5 1.3 collective-permute-start.13
  233.9 3.1 %collective-permute-done.13 = f32[3,4,2,12]{3,1,2,0:T(4,128)S(1)} collective-permute-done((f32[3,4,2,12]{3,1,2,0:T(4,128)S(1)}, f32[3,4,2,12]{3,1,2,0:T(4,128)S(1)}, u32[]{:S(2)}, u32[]{:S(2)}) %collective-permute-start.13) | collective-permute-done | bytes 1184 | tf_op jit(solution)/shard_map/ppermute | solution.py:25
  237.1 7.2 %collective-permute-start.14 = (f32[3,4,2,2]{3,1,2,0:T(4,128)S(1)}, f32[3,4,2,2]{3,1,2,0:T(4,128)S(1)}, u32[]{:S(2)}, u32[]{:S(2)}) collective-permute-start(f32[3,4,2,2]{3,1,2,0:T(4,128)S(1)} %get-tuple-element.100), channel_id=1, source_target_pairs={{0,2},{2,4},{4,6},{1,3},{3,5},{5,7},{8,10},{10,12},{12,14},{9,11},... | collective-permute-start | bytes 584 | tf_op jit(solution)/shard_map/ppermute | solution.py:24
  244.3 1.9 collective-permute-start.15
  246.5 2.8 %collective-permute-done.15 = f32[3,4,2,2]{3,1,2,0:T(4,128)S(1)} collective-permute-done((f32[3,4,2,2]{3,1,2,0:T(4,128)S(1)}, f32[3,4,2,2]{3,1,2,0:T(4,128)S(1)}, u32[]{:S(2)}, u32[]{:S(2)}) %collective-permute-start.15) | collective-permute-done | bytes 224 | tf_op jit(solution)/shard_map/ppermute | solution.py:25
  249.4 1.0 scatter-add.9
  (98 shorter events, 7.4 us)
Async XLA Ops:
  1.7 9.0 %collective-permute-start = (f32[32,12,128]{2,1,0:T(8,128)S(1)}, f32[32,12,128]{2,1,0:T(8,128)S(1)}, u32[]{:S(2)}, u32[]{:S(2)}) collective-permute-start(f32[32,12,128]{2,1,0:T(8,128)S(1)} %get-tuple-element.95), channel_id=1, source_target_pairs={{0,8},{8,16},{16,24},{1,9},{9,17},{17,25},{2,10},{10,18},{18,26},{... | collective-permute-start | bytes 589832 | tf_op jit(solution)/shard_map/ppermute | solution.py:24
  5.8 8.8 %collective-permute-start.1 = (f32[32,12,128]{2,1,0:T(8,128)S(1)}, f32[32,12,128]{2,1,0:T(8,128)S(1)}, u32[]{:S(2)}, u32[]{:S(2)}) collective-permute-start(f32[32,12,128]{2,1,0:T(8,128)S(1)} %get-tuple-element.96), channel_id=1, source_target_pairs={{8,0},{16,8},{24,16},{9,1},{17,9},{25,17},{10,2},{18,10},{26,18},{... | collective-permute-start | bytes 589832 | tf_op jit(solution)/shard_map/ppermute | solution.py:25
  16.6 10.9 %collective-permute-start.2 = (f32[32,32,12]{2,1,0:T(8,128)S(1)}, f32[32,32,12]{2,1,0:T(8,128)S(1)}, u32[]{:S(2)}, u32[]{:S(2)}) collective-permute-start(f32[32,32,12]{2,1,0:T(8,128)S(1)} %get-tuple-element.93), channel_id=1, source_target_pairs={{0,2},{2,4},{4,6},{1,3},{3,5},{5,7},{8,10},{10,12},{12,14},{9,11},... | collective-permute-start | bytes 147464 | tf_op jit(solution)/shard_map/ppermute | solution.py:24
  21.4 10.5 %collective-permute-start.3 = (f32[32,32,12]{2,1,0:T(8,128)S(1)}, f32[32,32,12]{2,1,0:T(8,128)S(1)}, u32[]{:S(2)}, u32[]{:S(2)}) collective-permute-start(f32[32,32,12]{2,1,0:T(8,128)S(1)} %get-tuple-element.94), channel_id=1, source_target_pairs={{2,0},{4,2},{6,4},{3,1},{5,3},{7,5},{10,8},{12,10},{14,12},{11,9},... | collective-permute-start | bytes 147464 | tf_op jit(solution)/shard_map/ppermute | solution.py:25
  32.4 6.2 %copy-start.4 = (s32[2,2,8]{2,1,0:T(2,128)S(1)}, s32[2,2,8]{2,1,0:T(2,128)}, u32[]{:S(2)}) copy-start(s32[2,2,8]{2,1,0:T(2,128)} %param.19) | copy-start | bytes 388
  33.7 6.7 %collective-permute-start.4 = (f32[12,32,128]{2,0,1:T(8,128)S(1)}, f32[12,32,128]{2,0,1:T(8,128)S(1)}, u32[]{:S(2)}, u32[]{:S(2)}) collective-permute-start(f32[12,32,128]{2,0,1:T(8,128)S(1)} %copy.50), channel_id=1, source_target_pairs={{0,1},{2,3},{4,5},{6,7},{8,9},{10,11},{12,13},{14,15},{16,17},{18,... | collective-permute-start | bytes 589832 | tf_op jit(solution)/shard_map/ppermute | solution.py:24
  37.3 7.1 %collective-permute-start.5 = (f32[12,32,128]{2,0,1:T(8,128)S(1)}, f32[12,32,128]{2,0,1:T(8,128)S(1)}, u32[]{:S(2)}, u32[]{:S(2)}) collective-permute-start(f32[12,32,128]{2,0,1:T(8,128)S(1)} %copy.51), channel_id=1, source_target_pairs={{1,0},{3,2},{5,4},{7,6},{9,8},{11,10},{13,12},{15,14},{17,16},{19,... | collective-permute-start | bytes 589832 | tf_op jit(solution)/shard_map/ppermute | solution.py:25
  45.2 2.8 %collective-permute-start.6 = (f32[2,32,128]{2,0,1:T(2,128)S(1)}, f32[2,32,128]{2,0,1:T(2,128)S(1)}, u32[]{:S(2)}, u32[]{:S(2)}) collective-permute-start(f32[2,32,128]{2,0,1:T(2,128)S(1)} %get-tuple-element.90), channel_id=1, source_target_pairs={{0,1},{2,3},{4,5},{6,7},{8,9},{10,11},{12,13},{14,15},{16,17},{18,... | collective-permute-start | bytes 98312 | tf_op jit(solution)/shard_map/ppermute | solution.py:24
  46.7 4.7 %collective-permute-start.7 = (f32[2,32,128]{2,0,1:T(2,128)S(1)}, f32[2,32,128]{2,0,1:T(2,128)S(1)}, u32[]{:S(2)}, u32[]{:S(2)}) collective-permute-start(f32[2,32,128]{2,0,1:T(2,128)S(1)} %get-tuple-element.89), channel_id=1, source_target_pairs={{1,0},{3,2},{5,4},{7,6},{9,8},{11,10},{13,12},{15,14},{17,16},{19,... | collective-permute-start | bytes 98312 | tf_op jit(solution)/shard_map/ppermute | solution.py:25
  51.3 11.9 %copy-start = (f32[32,32,128]{2,1,0:T(8,128)S(1)}, f32[32,32,128]{2,1,0:T(8,128)}, u32[]{:S(2)}) copy-start(f32[32,32,128]{2,1,0:T(8,128)} %param.17) | copy-start | bytes 1572868
  58.1 12.7 %collective-permute-start.8 = (f32[2,32,18,128]{3,1,2,0:T(8,128)}, f32[2,32,18,128]{3,1,2,0:T(8,128)S(1)}, u32[]{:S(2)}, u32[]{:S(2)}) collective-permute-start(f32[2,32,18,128]{3,1,2,0:T(8,128)} %get-tuple-element.87), channel_id=1, source_target_pairs={{0,8},{8,16},{16,24},{1,9},{9,17},{17,25},{2,10},{10,18},{18,26},{... | collective-permute-start | bytes 1769480 | tf_op jit(solution)/shard_map/ppermute | solution.py:24
  61.3 13.5 %collective-permute-start.9 = (f32[2,32,18,128]{3,1,2,0:T(8,128)}, f32[2,32,18,128]{3,1,2,0:T(8,128)S(1)}, u32[]{:S(2)}, u32[]{:S(2)}) collective-permute-start(f32[2,32,18,128]{3,1,2,0:T(8,128)} %get-tuple-element.88), channel_id=1, source_target_pairs={{8,0},{16,8},{24,16},{9,1},{17,9},{25,17},{10,2},{18,10},{26,18},{... | collective-permute-start | bytes 1769480 | tf_op jit(solution)/shard_map/ppermute | solution.py:25
  70.7 4.0 %copy-start.2 = (f32[2,32,18,128]{3,1,2,0:T(8,128)}, f32[2,32,18,128]{3,1,2,0:T(8,128)S(1)}, u32[]{:S(2)}) copy-start(f32[2,32,18,128]{3,1,2,0:T(8,128)S(1)} %collective-permute-done.8) | copy-start | bytes 1769476
  74.8 0.8 copy-start.3
  81.7 10.3 %collective-permute-start.10 = (f32[2,32,68,18]{2,1,3,0:T(8,128)}, f32[2,32,68,18]{2,1,3,0:T(8,128)}, u32[]{:S(2)}, u32[]{:S(2)}) collective-permute-start(f32[2,32,68,18]{2,1,3,0:T(8,128)} %copy.53), channel_id=1, source_target_pairs={{0,2},{2,4},{4,6},{1,3},{3,5},{5,7},{8,10},{10,12},{12,14},{9,11},... | collective-permute-start | bytes 940040 | tf_op jit(solution)/shard_map/ppermute | solution.py:24
  87.2 11.5 %collective-permute-start.11 = (f32[2,32,68,18]{2,1,3,0:T(8,128)}, f32[2,32,68,18]{2,1,3,0:T(8,128)}, u32[]{:S(2)}, u32[]{:S(2)}) collective-permute-start(f32[2,32,68,18]{2,1,3,0:T(8,128)} %copy.54), channel_id=1, source_target_pairs={{2,0},{4,2},{6,4},{3,1},{5,3},{7,5},{10,8},{12,10},{14,12},{11,9},... | collective-permute-start | bytes 940040 | tf_op jit(solution)/shard_map/ppermute | solution.py:25
  203.3 5.2 %copy-start.1 = (f32[32,32,128]{2,1,0:T(8,128)S(1)}, f32[32,32,128]{2,1,0:T(8,128)}, u32[]{:S(2)}) copy-start(f32[32,32,128]{2,1,0:T(8,128)} %param.17) | copy-start | bytes 1572868
  229.4 4.5 %collective-permute-start.12 = (f32[3,4,2,12]{3,1,2,0:T(4,128)S(1)}, f32[3,4,2,12]{3,1,2,0:T(4,128)S(1)}, u32[]{:S(2)}, u32[]{:S(2)}) collective-permute-start(f32[3,4,2,12]{3,1,2,0:T(4,128)S(1)} %get-tuple-element.97), channel_id=1, source_target_pairs={{0,8},{8,16},{16,24},{1,9},{9,17},{17,25},{2,10},{10,18},{18,26},{... | collective-permute-start | bytes 3464 | tf_op jit(solution)/shard_map/ppermute | solution.py:24
  232.5 4.4 %collective-permute-start.13 = (f32[3,4,2,12]{3,1,2,0:T(4,128)S(1)}, f32[3,4,2,12]{3,1,2,0:T(4,128)S(1)}, u32[]{:S(2)}, u32[]{:S(2)}) collective-permute-start(f32[3,4,2,12]{3,1,2,0:T(4,128)S(1)} %get-tuple-element.98), channel_id=1, source_target_pairs={{8,0},{16,8},{24,16},{9,1},{17,9},{25,17},{10,2},{18,10},{26,18},{... | collective-permute-start | bytes 3464 | tf_op jit(solution)/shard_map/ppermute | solution.py:25
  237.1 9.2 %collective-permute-start.14 = (f32[3,4,2,2]{3,1,2,0:T(4,128)S(1)}, f32[3,4,2,2]{3,1,2,0:T(4,128)S(1)}, u32[]{:S(2)}, u32[]{:S(2)}) collective-permute-start(f32[3,4,2,2]{3,1,2,0:T(4,128)S(1)} %get-tuple-element.100), channel_id=1, source_target_pairs={{0,2},{2,4},{4,6},{1,3},{3,5},{5,7},{8,10},{10,12},{12,14},{9,11},... | collective-permute-start | bytes 584 | tf_op jit(solution)/shard_map/ppermute | solution.py:24
  244.3 5.0 %collective-permute-start.15 = (f32[3,4,2,2]{3,1,2,0:T(4,128)S(1)}, f32[3,4,2,2]{3,1,2,0:T(4,128)S(1)}, u32[]{:S(2)}, u32[]{:S(2)}) collective-permute-start(f32[3,4,2,2]{3,1,2,0:T(4,128)S(1)} %get-tuple-element.99), channel_id=1, source_target_pairs={{2,0},{4,2},{6,4},{3,1},{5,3},{7,5},{10,8},{12,10},{14,12},{11,9},... | collective-permute-start | bytes 584 | tf_op jit(solution)/shard_map/ppermute | solution.py:25
where the time goes:
time: 252 us; the launch traced here: 251 us
  local copies, waits for them, and re-layouts  92.2 us (37%)
  waiting for transfers between devices  44.8 us (18%)
  other arithmetic  43.3 us (17%)
  starting transfers between devices  42.9 us (17%)
  matrix products  13.5 us (5%)
  blocking collectives  13.1 us (5%)
    gather x2, local copies, waits for them, and re-layouts, resample(): return fields[:, :, source_x, source_y]  49.1 us
    ppermute x8, starting transfers between devices, with_halo(): before = lax.ppermute(last, axis, up)  30.5 us
    ppermute x8, waiting for transfers between devices, with_halo(): after = lax.ppermute(leading, axis, down)  29.2 us
    select_n x1, local copies, waits for them, and re-layouts, shards(): fields = jnp.where(inside[None, None], fields, 0.0)  16.9 us
    ppermute x8, waiting for transfers between devices, with_halo(): before = lax.ppermute(last, axis, up)  15.6 us
    another operation x3, other arithmetic, spread(): return jnp.stack([value_field, slope_dx, slope_dy, slope_dz])  14.8 us
    ppermute x8, starting transfers between devices, with_halo(): after = lax.ppermute(leading, axis, down)  12.4 us
    add x2, other arithmetic, apply_taps(): running + weights[tap_num] * lax.slice_in_dim(volume, tap_num, tap_num +...  10.2 us
  transfers between devices with their start and end apart: 16, of which 13 were waited for; matrix products, arithmetic and copies ran while one was open for 4% of the time, Pallas kernels for 0%

commit v1 on v0

v1 whole, which is shorter than its diff:
```python
import functools
import math

import jax
import jax.numpy as jnp
import numpy as np
from jax import lax
from jax.experimental import pallas as pl
from jax.experimental.pallas import tpu as pltpu
from jax.sharding import PartitionSpec as P

BRICK = 16
RANGE = 16
EPSILON = 1e-06
SUPPORT_NORM = 64.0
LOG_POLE = math.log(2.0 + math.sqrt(3.0))
POLE = 2.0 - math.sqrt(3.0)
PAD = 32
HALO = RANGE + 2
F32 = jnp.float32
BF16 = jnp.bfloat16
MESH = pl.DeviceIdType.MESH
HIGHEST = lax.Precision.HIGHEST


def factor_table(length):
    t = np.arange(-PAD, length + PAD, dtype=np.float64) + 1.0
    inside = (t >= 1) & (t <= length)
    ti = np.clip(t, 1, length)
    scale = (1.0 / POLE - POLE) * (1.0 - POLE ** (2.0 * (length + 1)))
    low = 1.0 - POLE ** (2.0 * ti)
    high = 1.0 - POLE ** (2.0 * (length + 1 - ti))
    diag = 6.0 * low * high / scale
    fwd = -POLE * high / (1.0 - POLE ** (2.0 * (length + 2 - ti)))
    bwd = -POLE * low / (1.0 - POLE ** (2.0 * (ti + 1)))
    return [np.where(inside, v, 0.0) for v in (diag, fwd, bwd)]


def factor_tables(lengths):
    width = max(lengths) + 2 * PAD
    rows = []
    for length in lengths:
        for row in factor_table(length):
            rows.append(np.pad(row, (0, width - row.shape[0])))
    return np.stack(rows).astype(np.float32).reshape(-1), width


def inverse_entry(row, col, length):
    nearer = jnp.minimum(row, col).astype(F32) + 1.0
    farther = jnp.maximum(row, col).astype(F32) + 1.0
    entry = jnp.exp((nearer - farther) * LOG_POLE) * (1.0 - jnp.exp(-2.0 * LOG_POLE * nearer))
    entry = entry * (1.0 - jnp.exp(-2.0 * LOG_POLE * (length + 1 - farther)))
    entry = entry * (
        6.0 / ((1.0 / POLE - POLE) * (1.0 - math.exp(-2.0 * LOG_POLE * (length + 1))))
    )
    parity = 1.0 - 2.0 * ((row + col) & 1).astype(F32)
    return entry * parity


def iota(shape, dim):
    return lax.broadcasted_iota(jnp.int32, shape, dim)


def split3(left, right):
    left_hi = left.astype(BF16)
    left_lo = (left - left_hi.astype(F32)).astype(BF16)
    lhs = jnp.concatenate([left_hi, left_hi, left_lo], axis=1)
    return jnp.dot(lhs, right, preferred_element_type=F32)


def stack3(right):
    right_hi = right.astype(BF16)
    right_lo = (right - right_hi.astype(F32)).astype(BF16)
    return jnp.concatenate([right_hi, right_lo, right_hi], axis=0)


def bspline(offset):
    magnitude = jnp.abs(offset)
    inner = 2.0 / 3.0 - magnitude * magnitude + 0.5 * magnitude * magnitude * magnitude
    rest = jnp.maximum(2.0 - magnitude, 0.0)
    outer = rest * rest * rest / 6.0
    return jnp.where(magnitude < 1.0, inner, outer)


def taps_of(t):
    smooth = (
        (1.0 - t) * (1.0 - t) * (1.0 - t) / 6.0,
        (3.0 * t * t * t - 6.0 * t * t + 4.0) / 6.0,
        (-3.0 * t * t * t + 3.0 * t * t + 3.0 * t + 1.0) / 6.0,
        t * t * t / 6.0,
    )
    slope = (
        -((1.0 - t) * (1.0 - t)) / 2.0,
        (3.0 * t * t - 4.0 * t) / 2.0,
        (-3.0 * t * t + 2.0 * t + 1.0) / 2.0,
        t * t / 2.0,
    )
    return smooth, slope


def kernel(
    cfg, table, sub, off, img, fix, ncc_out, grad_out,
    uz, zrecv, cz, ux, xl, xr, ce, packl, packr, yl, yr, w0, w1, g0, g1, hs,
    ft, wv, px, py, pz, stat, statr, part, gather,
    s_send, s_recv, f_send, f_recv,
):
    (nx_dev, ny_dev, width_t, nz, nx, ny, dz, dx, dy, zp, ex) = cfg
    me_x, me_y, me_z = (lax.axis_index(a) for a in ("gx", "gy", "gz"))
    other_z = 1 - me_z
    start_x, start_y, start_z = me_x * dx, me_y * dy, me_z * dz
    nbx, nby = dx // BRICK, dy // BRICK

    peers = []
    for ix in (-1, 0, 1):
        for iy in (-1, 0, 1):
            for iz in (0, 1):
                if (ix, iy, iz) == (0, 0, 0):
                    continue
                px_, py_ = me_x + ix, me_y + iy
                ok = (px_ >= 0) & (px_ < nx_dev) & (py_ >= 0) & (py_ < ny_dev)
                target = (px_, py_, other_z if iz else me_z)
                peers.append((ix, iy, iz, ok, target))
    barrier = pltpu.get_barrier_semaphore()
    count = jnp.int32(0)
    for ix, iy, iz, ok, target in peers:
        @pl.when(ok)
        def _(target=target):
            pl.semaphore_signal(barrier, inc=1, device_id=target, device_id_type=MESH)
        count = count + ok.astype(jnp.int32)

    def coef(axis, kind, pos):
        return table[(3 * axis + kind) * width_t + PAD + pos]

    def local_solve(axis, start, length, load, store):
        state = None
        for r in range(length):
            term = coef(axis, 0, start + r) * load(r)
            state = term if state is None else term + coef(axis, 1, start + r) * state
            store(r, state)
        return None

    fwd = []
    state = None
    def zbody(i, state):
        state = coef(0, 0, start_z + i) * img[i] + coef(0, 1, start_z + i) * state
        uz[i] = state
        return state
    lax.fori_loop(0, dz, zbody, jnp.zeros((dx, dy), F32))
    def zback(i, state):
        r = dz - 1 - i
        state = coef(0, 2, start_z + r) * state
        uz[r] = uz[r] + state
        return state + coef(0, 0, start_z + r) * img[r]
    lax.fori_loop(0, dz, zback, jnp.zeros((dx, dy), F32))

    pl.semaphore_wait(barrier, count)
    first = jnp.where(me_z == 0, dz - 2, 0)
    z_copy = pltpu.make_async_remote_copy(
        src_ref=uz.at[pl.ds(first, 2)], dst_ref=zrecv, send_sem=s_send.at[0], recv_sem=s_recv.at[0],
        device_id=(me_x, me_y, other_z), device_id_type=MESH)
    z_copy.start()

    has_l, has_r = me_x > 0, me_x < nx_dev - 1
    has_d, has_u = me_y > 0, me_y < ny_dev - 1
    for have, ref in ((has_l, xl), (has_r, xr), (has_d, yl), (has_u, yr)):
        @pl.when(jnp.logical_not(have))
        def _(ref=ref):
            ref[...] = jnp.zeros(ref.shape, F32)

    tz, sz = taps_of(sub[0])
    tx, sx = taps_of(sub[1])
    ty, sy = taps_of(sub[2])
    lane = iota((1, dy), 1)
    group = lane // BRICK
    ox_v, oy_v = [], []
    for bx in range(nbx):
        vx = jnp.zeros((1, dy), jnp.int32)
        vy = jnp.zeros((1, dy), jnp.int32)
        for by in range(nby):
            vx = jnp.where(group == by, off[0, bx, by], vx)
            vy = jnp.where(group == by, off[1, bx, by], vy)
        ox_v.append(vx)
        oy_v.append(vy)

    nslot = dy // HALO
    col = iota((dy, 2 * dy), 1)
    src = iota((dy, 2 * dy), 0)
    lane_in = jnp.where(col < dy, col, col - dy)
    slot = lane_in // HALO
    at = lane_in - slot * HALO + jnp.where(col < dy, 0, dy - HALO)
    ends = jnp.where(slot < nslot, inverse_entry(start_y + at, start_y + src, ny), 0.0)

    wide = 2 * dy
    jcol = iota((dy, wide), 1) - HALO
    jin = (start_y + jcol >= 0) & (start_y + jcol < ny) & (jcol < dy + HALO)
    own_part = jnp.where(jin, inverse_entry(
        jnp.clip(start_y + jcol, 0, ny - 1), start_y + iota((dy, wide), 0), ny), 0.0)
    m = iota((dy, wide), 0)
    jf = (start_y + jcol + 1).astype(F32)
    parity = 1.0 - 2.0 * (jcol & 1).astype(F32)
    t_left = (start_y * jnp.ones((1, 1), jnp.int32)).astype(F32)
    t_right = t_left + float(dy + 1)
    high = 1.0 - jnp.exp(-2.0 * LOG_POLE * (ny + 1 - jf))
    low = 1.0 - jnp.exp(-2.0 * LOG_POLE * jf)
    jown = jcol.astype(F32)
    from_left = -parity * jnp.exp(-LOG_POLE * (jown + 1.0)) * high / (
        1.0 - jnp.exp(-2.0 * LOG_POLE * (ny + 1 - t_left)))
    from_right = parity * jnp.exp(LOG_POLE * (jown - float(dy))) * low / (
        1.0 - jnp.exp(-2.0 * LOG_POLE * t_right))
    if dy % 2:
        from_right = -from_right
    left_col = jnp.where(jcol < 0, jnp.where(m - HALO == jcol, 1.0, 0.0),
                         jnp.where(m == HALO - 1, from_left, 0.0))
    right_col = jnp.where(jcol >= dy, jnp.where(m - HALO + dy == jcol, 1.0, 0.0),
                          jnp.where(m == HALO, from_right, 0.0))
    halo_part = jnp.where(m < HALO, left_col, jnp.where(m < 2 * HALO, right_col, 0.0))
    halo_part = jnp.where(jin, halo_part, 0.0)
    full_y = jnp.concatenate([own_part, halo_part], axis=0)
    for bx, wref in ((0, w0), (1, w1)):
        jrow = iota((wide, dy), 0) - HALO
        want = lane + oy_v[bx]
        ok_y = jnp.where((start_y + want >= 0) & (start_y + want < ny), 1.0, 0.0)
        picks = []
        for taps in (ty, sy):
            acc = jnp.zeros((wide, dy), F32)
            for c in range(4):
                acc = jnp.where(jrow == want + (c - 1), taps[c], acc)
            picks.append(acc * ok_y)
        wref[...] = stack3(jnp.dot(full_y, jnp.concatenate(picks, axis=1), precision=HIGHEST,
                                   preferred_element_type=F32))

    ones = jnp.where(iota((dy, dy), 0) // BRICK == iota((dy, dy), 1) // BRICK, 1.0, 0.0)
    half = float(dz * BRICK * BRICK)

    def group_sum(rows):
        return jnp.dot(rows, ones, precision=HIGHEST, preferred_element_type=F32)

    def row8(vecs):
        rows = iota((8, dy), 0)
        out = jnp.zeros((8, dy), F32)
        for i, v in enumerate(vecs):
            out = jnp.where(rows == i, v, out)
        return out

    for i in range(dx // 8):
        ft[8 * i:8 * i + 8] = jnp.swapaxes(fix[:, 8 * i:8 * i + 8, :], 0, 1)
    fsum = [jnp.sum(jnp.sum(ft[BRICK * b:BRICK * b + BRICK], axis=0), axis=0, keepdims=True) for b in range(nbx)]
    mean_f = group_sum(row8(fsum)) / half
    sff = []
    for b in range(nbx):
        cf = ft[BRICK * b:BRICK * b + BRICK] - mean_f[b:b + 1][None]
        ft[BRICK * b:BRICK * b + BRICK] = cf
        sff.append(jnp.sum(jnp.sum(cf * cf, axis=0), axis=0, keepdims=True))

    z_copy.wait()
    left_on = jnp.where(me_z == 1, 1.0, 0.0)
    right_on = 1.0 - left_on
    zl = zrecv[1] * left_on
    zr0, zr1 = zrecv[0] * right_on, zrecv[1] * right_on
    def zf(i, y):
        y = coef(0, 1, start_z + i) * y
        cz[i + 1] = uz[i] + y
        return y
    lax.fori_loop(0, dz, zf, zl)
    y = coef(0, 1, start_z + dz) * cz[dz]
    cz[dz + 1] = zr0 + y
    y = coef(0, 1, start_z + dz + 1) * y
    cz[dz + 2] = zr1 + y
    def zb(i, y):
        r = dz - 1 - i
        y = coef(0, 2, start_z + r) * y
        cz[r + 1] = cz[r + 1] + y
        return y
    y = lax.fori_loop(0, dz, zb, zr0)
    cz[0] = zl + coef(0, 2, start_z - 1) * (uz[0] + y)
    for i in range(dz + 3, zp):
        cz[i] = jnp.zeros((dx, dy), F32)
    for i in range(dx // 8):
        ce[HALO - 1 + 8 * i:HALO - 1 + 8 * i + 8] = jnp.swapaxes(cz[:, 8 * i:8 * i + 8, :], 0, 1)

    def xf(i, y):
        y = coef(1, 0, start_x + i) * ce[HALO - 1 + i] + coef(1, 1, start_x + i) * y
        ux[i] = y
        return y
    lax.fori_loop(0, dx, xf, jnp.zeros((zp, dy), F32))
    def xb(i, y):
        r = dx - 1 - i
        y = coef(1, 2, start_x + r) * y
        ux[r] = ux[r] + y
        return y + coef(1, 0, start_x + r) * ce[HALO - 1 + r]
    lax.fori_loop(0, dx, xb, jnp.zeros((zp, dy), F32))

    def pair(low_src, low_dst, high_src, high_dst, sem, low_id, high_id, low_ok, high_ok):
        low = pltpu.make_async_remote_copy(
            src_ref=low_src, dst_ref=low_dst, send_sem=s_send.at[sem], recv_sem=s_recv.at[sem],
            device_id=low_id, device_id_type=MESH)
        high = pltpu.make_async_remote_copy(
            src_ref=high_src, dst_ref=high_dst, send_sem=s_send.at[sem + 1], recv_sem=s_recv.at[sem + 1],
            device_id=high_id, device_id_type=MESH)
        @pl.when(low_ok)
        def _():
            low.start()
        @pl.when(high_ok)
        def _():
            high.start()
        def wait():
            @pl.when(low_ok)
            def _():
                low.wait_send()
                high.wait_recv()
            @pl.when(high_ok)
            def _():
                high.wait_send()
                low.wait_recv()
        return wait

    wait_x = pair(ux.at[pl.ds(0, HALO)], xr, ux.at[pl.ds(dx - HALO, HALO)], xl, 1,
                  (me_x - 1, me_y, me_z), (me_x + 1, me_y, me_z), has_l, has_r)
    wait_x()
    def gf(i, y):
        y = coef(1, 1, start_x + i) * y
        ce[HALO - 1 + i] = ux[i] + y
        return y
    lax.fori_loop(0, dx, gf, xl[HALO - 1])
    def gr(i, y):
        y = coef(1, 1, start_x + dx + i) * y
        ce[HALO - 1 + dx + i] = xr[i] + y
        return y
    lax.fori_loop(0, HALO, gr, ce[HALO - 1 + dx - 1])
    def gb(i, y):
        r = dx - 1 - i
        y = coef(1, 2, start_x + r) * y
        ce[HALO - 1 + r] = ce[HALO - 1 + r] + y
        return y
    y = lax.fori_loop(0, dx, gb, xr[0])
    def gl(i, y):
        y = coef(1, 2, start_x - 1 - i) * y
        ce[HALO - 2 - i] = xl[HALO - 1 - i] + y
        return y
    lax.fori_loop(0, HALO - 1, gl, ux[0] + y)
    for i in range(dx + 2 * HALO - 1, ex):
        ce[i] = jnp.zeros((zp, dy), F32)

    rows = ex // nslot
    acc = jnp.zeros((rows * zp, 2 * dy), F32)
    for k in range(nslot):
        right = stack3(jnp.where(slot == k, ends, 0.0))
        acc = acc + split3(ce[rows * k:rows * k + rows].reshape(rows * zp, dy), right)
    packl[...] = acc[:, :dy].reshape(rows, zp, dy)
    packr[...] = acc[:, dy:].reshape(rows, zp, dy)
    wait_y = pair(packl, yr, packr, yl, 3,
                  (me_x, me_y - 1, me_z), (me_x, me_y + 1, me_z), has_d, has_u)
    wait_y()

    lane3 = iota((rows * zp, dy), 1)
    for k in range(nslot):
        own = ce[rows * k:rows * k + rows].reshape(rows * zp, dy)
        a = yl[...].reshape(rows * zp, dy)
        b = yr[...].reshape(rows * zp, dy)
        if k > 0:
            a = pltpu.roll(a, dy - HALO * k, 1)
        if k != 1:
            b = pltpu.roll(b, (dy + HALO - HALO * k) % dy, 1)
        halo = jnp.where(lane3 < HALO, a, jnp.where(lane3 < 2 * HALO, b, 0.0))
        both = jnp.concatenate([own, halo], axis=1)
        if k < nslot - 1:
            g0[rows * k:rows * k + rows] = split3(both, w0[...]).reshape(rows, zp, 2 * dy)
        if k > 0:
            g1[rows * (k - 1):rows * k] = split3(both, w1[...]).reshape(rows, zp, 2 * dy)

    group2 = jnp.concatenate([group, group], axis=1)
    wsum = []
    for bx, gref in ((0, g0), (1, g1)):
        base = [off[0, bx, by] + RANGE + bx * (BRICK - rows) for by in range(nby)]
        def pick(i, c, gref=gref, base=base):
            v = gref[base[0] + i]
            for by in range(1, nby):
                v = jnp.where(group2 == by, gref[base[by] + i], v)
            hs[i] = v
            return c
        lax.fori_loop(0, BRICK + 3, pick, 0)
        def fir(i, total, bx=bx):
            gx_pos = start_x + bx * BRICK + i + ox_v[bx]
            ok_x = jnp.where((gx_pos >= 0) & (gx_pos < nx), 1.0, 0.0)
            h = [hs[i + c] for c in range(4)]
            hv = [v[:, :dy] for v in h]
            hd = [v[:, dy:] for v in h]
            def comb(w, vs):
                return (w[0] * vs[0] + w[1] * vs[1] + w[2] * vs[2] + w[3] * vs[3]) * ok_x
            val, dxx, dyy = comb(tx, hv), comb(sx, hv), comb(tx, hd)
            def zfir(w, v):
                return w[0] * v[0:dz] + w[1] * v[1:dz + 1] + w[2] * v[2:dz + 2] + w[3] * v[3:dz + 3]
            out = zfir(tz, val)
            r = bx * BRICK + i
            wv[r] = out
            px[r] = zfir(tz, dxx)
            py[r] = zfir(tz, dyy)
            pz[r] = zfir(sz, val)
            return total + out
        total = lax.fori_loop(0, BRICK, fir, jnp.zeros((dz, dy), F32))
        wsum.append(jnp.sum(total, axis=0, keepdims=True))

    mean_w = group_sum(row8(wsum)) / half
    sww, sfw = [], []
    for b in range(nbx):
        cw = wv[BRICK * b:BRICK * b + BRICK] - mean_w[b:b + 1][None]
        wv[BRICK * b:BRICK * b + BRICK] = cw
        cf = ft[BRICK * b:BRICK * b + BRICK]
        sww.append(jnp.sum(jnp.sum(cw * cw, axis=0), axis=0, keepdims=True))
        sfw.append(jnp.sum(jnp.sum(cf * cw, axis=0), axis=0, keepdims=True))
    sums = group_sum(row8(sff + sww + sfw))
    stat[0] = row8([mean_f[b:b + 1] for b in range(nbx)] + [mean_w[b:b + 1] for b in range(nbx)])
    stat[1] = sums
    st_copy = pltpu.make_async_remote_copy(
        src_ref=stat, dst_ref=statr, send_sem=s_send.at[5], recv_sem=s_recv.at[5],
        device_id=(me_x, me_y, other_z), device_id_type=MESH)
    st_copy.start()
    st_copy.wait()
    voxels = 2.0 * half
    alphas, betas, gammas, nccs = [], [], [], []
    own_m, oth_m = stat[0], statr[0]
    own_s, oth_s = stat[1], statr[1]
    diff = own_m - oth_m
    for b in range(nbx):
        df, dw = diff[b:b + 1], diff[nbx + b:nbx + b + 1]
        def both_halves(i, extra):
            return own_s[i:i + 1] + oth_s[i:i + 1] + extra * (half / 2.0)
        ff = both_halves(b, df * df)
        ww = both_halves(nbx + b, dw * dw)
        fw = both_halves(2 * nbx + b, df * dw)
        inv = lax.rsqrt(ff * ww + EPSILON)
        ratio = fw / (ww + EPSILON)
        nccs.append(fw * inv)
        alphas.append(voxels * inv)
        betas.append(ratio)
        gammas.append(0.5 * (df - ratio * dw))
    every = jnp.where(iota((dy, dy), 0) == BRICK * iota((dy, dy), 1), 1.0, 0.0)
    ncc_rows = jnp.dot(row8(nccs), every, precision=HIGHEST, preferred_element_type=F32)
    ncc_out[...] = ncc_rows[:nbx, :nby]

    zrow = (start_z + iota((dz, 1), 0)).astype(F32)
    bz = [bspline((zrow - float(BRICK * k + BRICK // 2)) / BRICK) for k in range(nz // BRICK)]
    nk = nz // BRICK
    ne = nbx + 4
    ycol = iota((dy, dy), 1)
    yoff = (iota((dy, dy), 0) - BRICK * (ycol - 2) - BRICK // 2).astype(F32) / BRICK
    by_mat = jnp.where(ycol < nby + 4, bspline(yoff), 0.0)
    xrow = [[0.0] * dx for _ in range(ne)]
    for e in range(ne):
        for r in range(dx):
            u = abs(r - BRICK * (e - 2) - BRICK // 2) / BRICK
            xrow[e][r] = (2.0 / 3.0 - u * u + u ** 3 / 2.0) if u < 1 else max(2.0 - u, 0.0) ** 3 / 6.0
    for d, pref in enumerate((px, py, pz)):
        accs = [None] * ne
        for r in range(dx):
            b = r // BRICK
            g = alphas[b] * (ft[r] - betas[b] * wv[r] + gammas[b])
            force = g * pref[r]
            for e in range(ne):
                if xrow[e][r] != 0.0:
                    t = xrow[e][r] * force
                    accs[e] = t if accs[e] is None else accs[e] + t
        for e in range(ne):
            for k in range(nk):
                part[e, d * nk + k:d * nk + k + 1, :] = jnp.sum(accs[e] * bz[k], axis=0, keepdims=True)
    for e in range(ne):
        part[e, 3 * nk:] = jnp.zeros((part.shape[1] - 3 * nk, dy), F32)
    depth = part.shape[1]
    full = jnp.dot(part[...].reshape(ne * depth, dy), by_mat, precision=HIGHEST,
                   preferred_element_type=F32) * (1.0 / SUPPORT_NORM)
    part[...] = full.reshape(ne, depth, dy)

    def slot_of(ix, iy, iz):
        return ((ix + 1) * 3 + (iy + 1)) * 2 + iz

    for ix, iy, iz, ok, target in peers:
        there = slot_of(-ix, -iy, iz)
        here = slot_of(ix, iy, iz)
        @pl.when(jnp.logical_not(ok))
        def _(here=here):
            gather[here] = jnp.zeros(gather.shape[1:], F32)
        @pl.when(ok)
        def _(ix=ix, there=there, target=target):
            pltpu.make_async_remote_copy(
                src_ref=part.at[pl.ds(2 + nbx * ix if ix >= 0 else 0, nbx)] if nbx == 2 else None,
                dst_ref=gather.at[there], send_sem=f_send.at[there], recv_sem=f_recv.at[there],
                device_id=target, device_id_type=MESH).start()
    for ix, iy, iz, ok, target in peers:
        there = slot_of(-ix, -iy, iz)
        here = slot_of(ix, iy, iz)
        @pl.when(ok)
        def _(ix=ix, there=there, here=here, target=target):
            pltpu.make_async_remote_copy(
                src_ref=part.at[pl.ds(2 + nbx * ix if ix >= 0 else 0, nbx)],
                dst_ref=gather.at[there], send_sem=f_send.at[there], recv_sem=f_recv.at[there],
                device_id=target, device_id_type=MESH).wait_send()
            pltpu.make_async_remote_copy(
                src_ref=part.at[pl.ds(0, nbx)],
                dst_ref=gather.at[here], send_sem=f_send.at[here], recv_sem=f_recv.at[here],
                device_id=target, device_id_type=MESH).wait_recv()
    gather_own = part[2:2 + nbx]
    lane_c = iota((nbx * depth, dy), 1)
    result = None
    for iy in (-1, 0, 1):
        total = gather_own if iy == 0 else None
        for ix in (-1, 0, 1):
            for iz in (0, 1):
                if (ix, iy, iz) == (0, 0, 0):
                    continue
                v = gather[slot_of(ix, iy, iz)]
                total = v if total is None else total + v
        total = total.reshape(nbx * depth, dy)
        if iy == 0:
            moved = pltpu.roll(total, dy - 2, 1)
        elif iy < 0:
            moved = jnp.where(lane_c < 2, pltpu.roll(total, dy - (nby + 2), 1), 0.0)
        else:
            moved = jnp.where(lane_c >= nby - 2, pltpu.roll(total, nby - 2, 1), 0.0)
        result = moved if result is None else result + moved
    for i in range(nbx):
        for d in range(3):
            for k in range(nk):
                row = i * depth + d * nk + k
                grad_out[d, k, i:i + 1, :] = result[row:row + 1, :nby]


def shards(sizes, moving_image, fixed_image, subvoxel, brick_offset):
    nx_dev, ny_dev, nz_dev = sizes
    dz, dx, dy = moving_image.shape
    nz, nx, ny = dz * nz_dev, dx * nx_dev, dy * ny_dev
    table, width_t = factor_tables((nz, nx, ny))
    zp = -(-(dz + 3) // 8) * 8
    nslot = dy // HALO
    ex = -(-(dx + 2 * HALO - 1) // nslot) * nslot
    rows = ex // nslot
    nbx, nby, nk = dx // BRICK, dy // BRICK, nz // BRICK
    depth = -(-3 * nk // 8) * 8
    cfg = (nx_dev, ny_dev, width_t, nz, nx, ny, dz, dx, dy, zp, ex)
    vm = lambda *shape: pltpu.VMEM(shape, F32)
    vspec = pl.BlockSpec(memory_space=pltpu.VMEM)
    sspec = pl.BlockSpec(memory_space=pltpu.SMEM)
    return pl.pallas_call(
        functools.partial(kernel, cfg),
        out_shape=(
            jax.ShapeDtypeStruct((nbx, nby), F32),
            jax.ShapeDtypeStruct((3, nk, nbx, nby), F32),
        ),
        in_specs=[sspec, sspec, sspec, vspec, vspec],
        out_specs=(vspec, vspec),
        scratch_shapes=[
            vm(dz, dx, dy), vm(2, dx, dy), vm(zp, dx, dy),
            vm(dx, zp, dy), vm(HALO, zp, dy), vm(HALO, zp, dy), vm(ex, zp, dy),
            vm(rows, zp, dy), vm(rows, zp, dy), vm(rows, zp, dy), vm(rows, zp, dy),
            pltpu.VMEM((6 * dy, 2 * dy), BF16), pltpu.VMEM((6 * dy, 2 * dy), BF16),
            vm(ex - rows, zp, 2 * dy), vm(ex - rows, zp, 2 * dy), vm(BRICK + 3, zp, 2 * dy),
            vm(dx, dz, dy), vm(dx, dz, dy), vm(dx, dz, dy), vm(dx, dz, dy), vm(dx, dz, dy),
            vm(2, 8, dy), vm(2, 8, dy),
            vm(nbx + 4, depth, dy), vm(18, nbx, depth, dy),
            pltpu.SemaphoreType.DMA((6,)), pltpu.SemaphoreType.DMA((6,)),
            pltpu.SemaphoreType.DMA((18,)), pltpu.SemaphoreType.DMA((18,)),
        ],
        compiler_params=pltpu.CompilerParams(
            collective_id=0, has_side_effects=True, vmem_limit_bytes=56 * 1024 * 1024),
    )(jnp.asarray(table), subvoxel, brick_offset, moving_image, fixed_image)


def solution(mesh):
    sizes = (mesh.shape["gx"], mesh.shape["gy"], mesh.shape["gz"])
    return jax.shard_map(
        functools.partial(shards, sizes),
        mesh=mesh,
        in_specs=(P("gz", "gx", "gy"), P("gz", "gx", "gy"), P(), P(None, "gx", "gy")),
        out_specs=(P("gx", "gy"), P(None, None, "gx", "gy")),
        check_vma=False,
    )
```

time: 252 us -> 44 us (0.17)
  local copies, waits for them, and re-layouts: 92.2 us -> 2.53 us
  waiting for transfers between devices: 44.8 us -> 0 us
  other arithmetic: 43.3 us -> 0 us
  starting transfers between devices: 42.9 us -> 0 us
  Pallas kernels: 0 us -> 40.6 us
  matrix products: 13.5 us -> 0 us
  blocking collectives: 13.1 us -> 0 us
    gather x2 -> x0, local copies, waits for them, and re-layouts: 49.1 us -> none  [resample(): return fields[:, :, source_x, source_y]]
    ppermute x16 -> x0, waiting for transfers between devices: 44.8 us -> none  [the longest x8 29.2 us: with_halo(): after = lax.ppermute(leading, axis, down)]
    ppermute x16 -> x0, starting transfers between devices: 42.9 us -> none  [the longest x8 30.5 us: with_halo(): before = lax.ppermute(last, axis, up)]
    pallas_call x0 -> x1, Pallas kernels: none -> 40.6 us  [shards(): pl.pallas_call(functools.partial(kernel, cfg), out_shape=(jax.ShapeDtypeS...]
    another operation x7 -> x0, other arithmetic: 22.2 us -> none  [the longest x3 14.8 us: spread(): return jnp.stack([value_field, slope_dx, slope_dy, slope_dz])]
    select_n x1 -> x0, local copies, waits for them, and re-layouts: 16.9 us -> none  [shards(): fields = jnp.where(inside[None, None], fields, 0.0)]
    dot_general x6 -> x0, matrix products: 13.5 us -> none  [the longest x1 6.22 us: shards(): jnp.einsum('dzxy,jy->dzxj', forces, basis_y, precision=lax.Precision.HIGH...]
    psum x3 -> x0, blocking collectives: 13.1 us -> none  [the longest x1 5.35 us: shards(): summed = lax.psum(partial_z, 'gz')]
  transfers between devices with their start and end apart: 16 -> 0, of which waited for: 13 -> 0; matrix products, arithmetic and copies ran while one was open for 4% -> 0% of each run, Pallas kernels for 0% -> 0%
where the time goes in v1:
time: 44 us; the launch traced here: 43.7 us
  Pallas kernels  40.6 us (92%)
  local copies, waits for them, and re-layouts  2.53 us (6%)
  between operations  0.65 us (1%)
    pallas_call x1, Pallas kernels, shards(): pl.pallas_call(functools.partial(kernel, cfg), out_shape=(jax.ShapeDtypeS...  40.6 us
    unnamed x4, local copies, waits for them, and re-layouts  2.53 us

profile of v1, /device:TPU:1, one launch (start us, length us, event | category | flops | bytes accessed | tf_op | source)
XLA Modules:
  0.0 43.7 jit_solution(12312877683338820987)
XLA Ops:
  0.6 40.6 %shard_map.68 = (f32[2,8]{1,0:T(2,128)}, f32[3,4,2,8]{3,2,1,0:T(2,128)}) custom-call(f32[5184]{0:T(1024)} %constant.2.clone.table, f32[3]{0:T(128)} %sub.1, s32[2,2,8]{2,1,0:T(2,128)} %off.1, f32[32,32,128]{2,1,0:T(8,128)} %img.1, f32[32,32,128]{2,1,0:T(8,128)} %fix.1), custom_call_target="tpu_custom_call" | custom-call | tf_op jit(solution)/shard_map/pallas_call | solution.py:542
  41.2 0.0 copy-start
  41.2 0.7 %copy-done = f32[2,8]{1,0:T(2,128)S(1)} copy-done((f32[2,8]{1,0:T(2,128)S(1)}, f32[2,8]{1,0:T(2,128)}, u32[]{:S(2)}) %copy-start) | copy-done | bytes 88
  41.9 0.6 %copy.9 = f32[2,8]{1,0:T(2,128)} copy(f32[2,8]{1,0:T(2,128)S(1)} %copy-done) | data formatting | bytes 128
  42.4 1.3 %copy.10 = f32[3,4,2,8]{3,2,1,0:T(2,128)} copy(f32[3,4,2,8]{3,2,1,0:T(2,128)} %get-tuple-element.5) | data formatting | bytes 1536
Async XLA Ops:
  41.2 0.7 %copy-start = (f32[2,8]{1,0:T(2,128)S(1)}, f32[2,8]{1,0:T(2,128)}, u32[]{:S(2)}) copy-start(f32[2,8]{1,0:T(2,128)} %get-tuple-element.4) | copy-start | bytes 196

commit v2 on v1

--- a/solution.py
+++ b/solution.py
@@ -99,9 +99,9 @@
 
 
 def kernel(
-    cfg, table, sub, off, img, fix, ncc_out, grad_out,
-    uz, zrecv, cz, ux, xl, xr, ce, packl, packr, yl, yr, w0, w1, g0, g1, hs,
-    ft, wv, px, py, pz, stat, statr, part, gather,
+    cfg, table, sub, off, img_hbm, fix_hbm, ncc_out, grad_out,
+    img, fix, in_sem, uz, zrecv, cz, ux, xl, xr, ce, packl, packr, yl, yr, ends3, w0, w1, g0, g1, hs,
+    ft, wv, px, py, pz, proj, stat, statr, part, gather,
     s_send, s_recv, f_send, f_recv,
 ):
     (nx_dev, ny_dev, width_t, nz, nx, ny, dz, dx, dy, zp, ex) = cfg
@@ -109,6 +109,11 @@
     other_z = 1 - me_z
     start_x, start_y, start_z = me_x * dx, me_y * dy, me_z * dz
     nbx, nby = dx // BRICK, dy // BRICK
+
+    load_img = pltpu.make_async_copy(img_hbm, img, in_sem.at[0])
+    load_fix = pltpu.make_async_copy(fix_hbm, fix, in_sem.at[1])
+    load_img.start()
+    load_fix.start()
 
     peers = []
     for ix in (-1, 0, 1):
@@ -123,6 +128,8 @@
     barrier = pltpu.get_barrier_semaphore()
     count = jnp.int32(0)
     for ix, iy, iz, ok, target in peers:
+        if abs(ix) + abs(iy) + iz > 1:
+            continue
         @pl.when(ok)
         def _(target=target):
             pl.semaphore_signal(barrier, inc=1, device_id=target, device_id_type=MESH)
@@ -131,27 +138,18 @@
     def coef(axis, kind, pos):
         return table[(3 * axis + kind) * width_t + PAD + pos]
 
-    def local_solve(axis, start, length, load, store):
-        state = None
-        for r in range(length):
-            term = coef(axis, 0, start + r) * load(r)
-            state = term if state is None else term + coef(axis, 1, start + r) * state
-            store(r, state)
-        return None
-
-    fwd = []
-    state = None
+    load_img.wait()
     def zbody(i, state):
         state = coef(0, 0, start_z + i) * img[i] + coef(0, 1, start_z + i) * state
         uz[i] = state
         return state
-    lax.fori_loop(0, dz, zbody, jnp.zeros((dx, dy), F32))
+    lax.fori_loop(0, dz, zbody, jnp.zeros((dx, dy), F32), unroll=True)
     def zback(i, state):
         r = dz - 1 - i
         state = coef(0, 2, start_z + r) * state
         uz[r] = uz[r] + state
         return state + coef(0, 0, start_z + r) * img[r]
-    lax.fori_loop(0, dz, zback, jnp.zeros((dx, dy), F32))
+    lax.fori_loop(0, dz, zback, jnp.zeros((dx, dy), F32), unroll=True)
 
     pl.semaphore_wait(barrier, count)
     first = jnp.where(me_z == 0, dz - 2, 0)
@@ -188,7 +186,7 @@
     lane_in = jnp.where(col < dy, col, col - dy)
     slot = lane_in // HALO
     at = lane_in - slot * HALO + jnp.where(col < dy, 0, dy - HALO)
-    ends = jnp.where(slot < nslot, inverse_entry(start_y + at, start_y + src, ny), 0.0)
+    ends3[...] = stack3(jnp.where(slot == 0, inverse_entry(start_y + at, start_y + src, ny), 0.0))
 
     wide = 2 * dy
     jcol = iota((dy, wide), 1) - HALO
@@ -242,6 +240,7 @@
             out = jnp.where(rows == i, v, out)
         return out
 
+    load_fix.wait()
     for i in range(dx // 8):
         ft[8 * i:8 * i + 8] = jnp.swapaxes(fix[:, 8 * i:8 * i + 8, :], 0, 1)
     fsum = [jnp.sum(jnp.sum(ft[BRICK * b:BRICK * b + BRICK], axis=0), axis=0, keepdims=True) for b in range(nbx)]
@@ -261,7 +260,7 @@
         y = coef(0, 1, start_z + i) * y
         cz[i + 1] = uz[i] + y
         return y
-    lax.fori_loop(0, dz, zf, zl)
+    lax.fori_loop(0, dz, zf, zl, unroll=True)
     y = coef(0, 1, start_z + dz) * cz[dz]
     cz[dz + 1] = zr0 + y
     y = coef(0, 1, start_z + dz + 1) * y
@@ -271,7 +270,7 @@
         y = coef(0, 2, start_z + r) * y
         cz[r + 1] = cz[r + 1] + y
         return y
-    y = lax.fori_loop(0, dz, zb, zr0)
+    y = lax.fori_loop(0, dz, zb, zr0, unroll=True)
     cz[0] = zl + coef(0, 2, start_z - 1) * (uz[0] + y)
     for i in range(dz + 3, zp):
         cz[i] = jnp.zeros((dx, dy), F32)
@@ -282,13 +281,13 @@
         y = coef(1, 0, start_x + i) * ce[HALO - 1 + i] + coef(1, 1, start_x + i) * y
         ux[i] = y
         return y
-    lax.fori_loop(0, dx, xf, jnp.zeros((zp, dy), F32))
+    lax.fori_loop(0, dx, xf, jnp.zeros((zp, dy), F32), unroll=True)
     def xb(i, y):
         r = dx - 1 - i
         y = coef(1, 2, start_x + r) * y
         ux[r] = ux[r] + y
         return y + coef(1, 0, start_x + r) * ce[HALO - 1 + r]
-    lax.fori_loop(0, dx, xb, jnp.zeros((zp, dy), F32))
+    lax.fori_loop(0, dx, xb, jnp.zeros((zp, dy), F32), unroll=True)
 
     def pair(low_src, low_dst, high_src, high_dst, sem, low_id, high_id, low_ok, high_ok):
         low = pltpu.make_async_remote_copy(
@@ -314,59 +313,85 @@
                 low.wait_recv()
         return wait
 
-    wait_x = pair(ux.at[pl.ds(0, HALO)], xr, ux.at[pl.ds(dx - HALO, HALO)], xl, 1,
-                  (me_x - 1, me_y, me_z), (me_x + 1, me_y, me_z), has_l, has_r)
-    wait_x()
-    def gf(i, y):
-        y = coef(1, 1, start_x + i) * y
-        ce[HALO - 1 + i] = ux[i] + y
-        return y
-    lax.fori_loop(0, dx, gf, xl[HALO - 1])
-    def gr(i, y):
-        y = coef(1, 1, start_x + dx + i) * y
-        ce[HALO - 1 + dx + i] = xr[i] + y
-        return y
-    lax.fori_loop(0, HALO, gr, ce[HALO - 1 + dx - 1])
-    def gb(i, y):
-        r = dx - 1 - i
-        y = coef(1, 2, start_x + r) * y
-        ce[HALO - 1 + r] = ce[HALO - 1 + r] + y
-        return y
-    y = lax.fori_loop(0, dx, gb, xr[0])
-    def gl(i, y):
-        y = coef(1, 2, start_x - 1 - i) * y
-        ce[HALO - 2 - i] = xl[HALO - 1 - i] + y
-        return y
-    lax.fori_loop(0, HALO - 1, gl, ux[0] + y)
+    nch = zp // 8
+    rows = ex // nslot
     for i in range(dx + 2 * HALO - 1, ex):
         ce[i] = jnp.zeros((zp, dy), F32)
-
-    rows = ex // nslot
-    acc = jnp.zeros((rows * zp, 2 * dy), F32)
-    for k in range(nslot):
-        right = stack3(jnp.where(slot == k, ends, 0.0))
-        acc = acc + split3(ce[rows * k:rows * k + rows].reshape(rows * zp, dy), right)
-    packl[...] = acc[:, :dy].reshape(rows, zp, dy)
-    packr[...] = acc[:, dy:].reshape(rows, zp, dy)
-    wait_y = pair(packl, yr, packr, yl, 3,
-                  (me_x, me_y - 1, me_z), (me_x, me_y + 1, me_z), has_d, has_u)
-    wait_y()
-
-    lane3 = iota((rows * zp, dy), 1)
-    for k in range(nslot):
-        own = ce[rows * k:rows * k + rows].reshape(rows * zp, dy)
-        a = yl[...].reshape(rows * zp, dy)
-        b = yr[...].reshape(rows * zp, dy)
-        if k > 0:
-            a = pltpu.roll(a, dy - HALO * k, 1)
-        if k != 1:
-            b = pltpu.roll(b, (dy + HALO - HALO * k) % dy, 1)
-        halo = jnp.where(lane3 < HALO, a, jnp.where(lane3 < 2 * HALO, b, 0.0))
-        both = jnp.concatenate([own, halo], axis=1)
-        if k < nslot - 1:
-            g0[rows * k:rows * k + rows] = split3(both, w0[...]).reshape(rows, zp, 2 * dy)
-        if k > 0:
-            g1[rows * (k - 1):rows * k] = split3(both, w1[...]).reshape(rows, zp, 2 * dy)
+    waits_x, waits_y = [], []
+    for c in range(nch):
+        zs = pl.ds(8 * c, 8)
+        waits_x.append(pair(
+            ux.at[pl.ds(0, HALO), zs], xr.at[:, zs], ux.at[pl.ds(dx - HALO, HALO), zs], xl.at[:, zs],
+            6 + 2 * c, (me_x - 1, me_y, me_z), (me_x + 1, me_y, me_z), has_l, has_r))
+
+    def combine(c):
+        zs = pl.ds(8 * c, 8)
+        def gf(i, y):
+            y = coef(1, 1, start_x + i) * y
+            ce[HALO - 1 + i, zs] = ux[i, zs] + y
+            return y
+        lax.fori_loop(0, dx, gf, xl[HALO - 1, zs], unroll=True)
+        def gr(i, y):
+            y = coef(1, 1, start_x + dx + i) * y
+            ce[HALO - 1 + dx + i, zs] = xr[i, zs] + y
+            return y
+        lax.fori_loop(0, HALO, gr, ce[HALO - 1 + dx - 1, zs], unroll=True)
+        def gb(i, y):
+            r = dx - 1 - i
+            y = coef(1, 2, start_x + r) * y
+            ce[HALO - 1 + r, zs] = ce[HALO - 1 + r, zs] + y
+            return y
+        y = lax.fori_loop(0, dx, gb, xr[0, zs], unroll=True)
+        def gl(i, y):
+            y = coef(1, 2, start_x - 1 - i) * y
+            ce[HALO - 2 - i, zs] = xl[HALO - 1 - i, zs] + y
+            return y
+        lax.fori_loop(0, HALO - 1, gl, ux[0, zs] + y, unroll=True)
+
+    n8 = rows * 8
+    def pack(c):
+        res = split3(ce[:, 8 * c:8 * c + 8, :].reshape(ex * 8, dy), ends3[...])
+        low, high = None, None
+        for k in range(nslot):
+            a = res[n8 * k:n8 * k + n8, :dy]
+            b = res[n8 * k:n8 * k + n8, dy:]
+            if k > 0:
+                a = pltpu.roll(a, HALO * k, 1)
+                b = pltpu.roll(b, HALO * k, 1)
+            low = a if low is None else low + a
+            high = b if high is None else high + b
+        packl[c] = low.reshape(rows, 8, dy)
+        packr[c] = high.reshape(rows, 8, dy)
+
+    lane3 = iota((n8, dy), 1)
+    def spread_y(c):
+        left = yl[c].reshape(n8, dy)
+        right = yr[c].reshape(n8, dy)
+        halos = []
+        for k in range(nslot):
+            a, b = left, right
+            if k > 0:
+                a = pltpu.roll(a, dy - HALO * k, 1)
+            if k != 1:
+                b = pltpu.roll(b, (dy + HALO - HALO * k) % dy, 1)
+            halos.append(jnp.where(lane3 < HALO, a, jnp.where(lane3 < 2 * HALO, b, 0.0)))
+        own = ce[:, 8 * c:8 * c + 8, :].reshape(ex * 8, dy)
+        both = jnp.concatenate([own, jnp.concatenate(halos, axis=0)], axis=1)
+        count = (ex - rows) * 8
+        g0[:, 8 * c:8 * c + 8, :] = split3(both[:count], w0[...]).reshape(ex - rows, 8, 2 * dy)
+        g1[:, 8 * c:8 * c + 8, :] = split3(both[n8:], w1[...]).reshape(ex - rows, 8, 2 * dy)
+
+    for c in range(nch):
+        waits_x[c]()
+        combine(c)
+        pack(c)
+        waits_y.append(pair(packl.at[c], yr.at[c], packr.at[c], yl.at[c], 6 + 2 * nch + 2 * c,
+                            (me_x, me_y - 1, me_z), (me_x, me_y + 1, me_z), has_d, has_u))
+        if c > 0:
+            waits_y[c - 1]()
+            spread_y(c - 1)
+    waits_y[nch - 1]()
+    spread_y(nch - 1)
 
     group2 = jnp.concatenate([group, group], axis=1)
     wsum = []
@@ -415,6 +440,25 @@
         src_ref=stat, dst_ref=statr, send_sem=s_send.at[5], recv_sem=s_recv.at[5],
         device_id=(me_x, me_y, other_z), device_id_type=MESH)
     st_copy.start()
+
+    ne = nbx + 4
+    xrow = [[0.0] * dx for _ in range(ne)]
+    for e in range(ne):
+        for r in range(dx):
+            u = abs(r - BRICK * (e - 2) - BRICK // 2) / BRICK
+            xrow[e][r] = (2.0 / 3.0 - u * u + u ** 3 / 2.0) if u < 1 else max(2.0 - u, 0.0) ** 3 / 6.0
+    for d, pref in enumerate((px, py, pz)):
+        for b in range(nbx):
+            for kind, other in enumerate((ft, wv, None)):
+                accs = [None] * 5
+                for r in range(BRICK * b, BRICK * b + BRICK):
+                    force = pref[r] if other is None else pref[r] * other[r]
+                    for e in range(5):
+                        if xrow[b + e][r] != 0.0:
+                            t = xrow[b + e][r] * force
+                            accs[e] = t if accs[e] is None else accs[e] + t
+                for e in range(5):
+                    proj[((d * nbx + b) * 3 + kind) * 5 + e] = accs[e]
     st_copy.wait()
     voxels = 2.0 * half
     alphas, betas, gammas, nccs = [], [], [], []
@@ -441,25 +485,16 @@
     zrow = (start_z + iota((dz, 1), 0)).astype(F32)
     bz = [bspline((zrow - float(BRICK * k + BRICK // 2)) / BRICK) for k in range(nz // BRICK)]
     nk = nz // BRICK
-    ne = nbx + 4
     ycol = iota((dy, dy), 1)
     yoff = (iota((dy, dy), 0) - BRICK * (ycol - 2) - BRICK // 2).astype(F32) / BRICK
     by_mat = jnp.where(ycol < nby + 4, bspline(yoff), 0.0)
-    xrow = [[0.0] * dx for _ in range(ne)]
-    for e in range(ne):
-        for r in range(dx):
-            u = abs(r - BRICK * (e - 2) - BRICK // 2) / BRICK
-            xrow[e][r] = (2.0 / 3.0 - u * u + u ** 3 / 2.0) if u < 1 else max(2.0 - u, 0.0) ** 3 / 6.0
-    for d, pref in enumerate((px, py, pz)):
+    for d in range(3):
         accs = [None] * ne
-        for r in range(dx):
-            b = r // BRICK
-            g = alphas[b] * (ft[r] - betas[b] * wv[r] + gammas[b])
-            force = g * pref[r]
-            for e in range(ne):
-                if xrow[e][r] != 0.0:
-                    t = xrow[e][r] * force
-                    accs[e] = t if accs[e] is None else accs[e] + t
+        for b in range(nbx):
+            for e in range(5):
+                at3 = ((d * nbx + b) * 3) * 5 + e
+                t = alphas[b] * (proj[at3] - betas[b] * proj[at3 + 5] + gammas[b] * proj[at3 + 10])
+                accs[b + e] = t if accs[b + e] is None else accs[b + e] + t
         for e in range(ne):
             for k in range(nk):
                 part[e, d * nk + k:d * nk + k + 1, :] = jnp.sum(accs[e] * bz[k], axis=0, keepdims=True)
@@ -482,7 +517,7 @@
         @pl.when(ok)
         def _(ix=ix, there=there, target=target):
             pltpu.make_async_remote_copy(
-                src_ref=part.at[pl.ds(2 + nbx * ix if ix >= 0 else 0, nbx)] if nbx == 2 else None,
+                src_ref=part.at[pl.ds(2 + nbx * ix if ix >= 0 else 0, nbx)],
                 dst_ref=gather.at[there], send_sem=f_send.at[there], recv_sem=f_recv.at[there],
                 device_id=target, device_id_type=MESH).start()
     for ix, iy, iz, ok, target in peers:
@@ -533,11 +568,13 @@
     nslot = dy // HALO
     ex = -(-(dx + 2 * HALO - 1) // nslot) * nslot
     rows = ex // nslot
+    nch = zp // 8
     nbx, nby, nk = dx // BRICK, dy // BRICK, nz // BRICK
     depth = -(-3 * nk // 8) * 8
     cfg = (nx_dev, ny_dev, width_t, nz, nx, ny, dz, dx, dy, zp, ex)
     vm = lambda *shape: pltpu.VMEM(shape, F32)
     vspec = pl.BlockSpec(memory_space=pltpu.VMEM)
+    hspec = pl.BlockSpec(memory_space=pl.ANY)
     sspec = pl.BlockSpec(memory_space=pltpu.SMEM)
     return pl.pallas_call(
         functools.partial(kernel, cfg),
@@ -545,18 +582,21 @@
             jax.ShapeDtypeStruct((nbx, nby), F32),
             jax.ShapeDtypeStruct((3, nk, nbx, nby), F32),
         ),
-        in_specs=[sspec, sspec, sspec, vspec, vspec],
+        in_specs=[sspec, sspec, sspec, hspec, hspec],
         out_specs=(vspec, vspec),
         scratch_shapes=[
+            vm(dz, dx, dy), vm(dz, dx, dy), pltpu.SemaphoreType.DMA((2,)),
             vm(dz, dx, dy), vm(2, dx, dy), vm(zp, dx, dy),
             vm(dx, zp, dy), vm(HALO, zp, dy), vm(HALO, zp, dy), vm(ex, zp, dy),
-            vm(rows, zp, dy), vm(rows, zp, dy), vm(rows, zp, dy), vm(rows, zp, dy),
+            vm(nch, rows, 8, dy), vm(nch, rows, 8, dy), vm(nch, rows, 8, dy), vm(nch, rows, 8, dy),
+            pltpu.VMEM((3 * dy, 2 * dy), BF16),
             pltpu.VMEM((6 * dy, 2 * dy), BF16), pltpu.VMEM((6 * dy, 2 * dy), BF16),
             vm(ex - rows, zp, 2 * dy), vm(ex - rows, zp, 2 * dy), vm(BRICK + 3, zp, 2 * dy),
             vm(dx, dz, dy), vm(dx, dz, dy), vm(dx, dz, dy), vm(dx, dz, dy), vm(dx, dz, dy),
+            vm(3 * nbx * 3 * 5, dz, dy),
             vm(2, 8, dy), vm(2, 8, dy),
             vm(nbx + 4, depth, dy), vm(18, nbx, depth, dy),
-            pltpu.SemaphoreType.DMA((6,)), pltpu.SemaphoreType.DMA((6,)),
+            pltpu.SemaphoreType.DMA((6 + 4 * nch,)), pltpu.SemaphoreType.DMA((6 + 4 * nch,)),
             pltpu.SemaphoreType.DMA((18,)), pltpu.SemaphoreType.DMA((18,)),
         ],
         compiler_params=pltpu.CompilerParams(

time: 44 us -> 38.8 us (0.88)
  Pallas kernels: 40.6 us -> 35.3 us
    pallas_call x1, Pallas kernels: 40.6 us -> 35.3 us  [shards(): pl.pallas_call(functools.partial(kernel, cfg), out_shape=(jax.ShapeDtypeS...]
where the time goes in v2:
time: 38.8 us; the launch traced here: 38.5 us
  Pallas kernels  35.3 us (91%)
  local copies, waits for them, and re-layouts  2.53 us (7%)
  between operations  0.65 us (2%)
    pallas_call x1, Pallas kernels, shards(): pl.pallas_call(functools.partial(kernel, cfg), out_shape=(jax.ShapeDtypeS...  35.3 us
    unnamed x4, local copies, waits for them, and re-layouts  2.53 us

profile of v2, /device:TPU:1, one launch (start us, length us, event | category | flops | bytes accessed | tf_op | source)
XLA Modules:
  0.0 38.5 jit_solution(18147079186071101779)
XLA Ops:
  0.6 35.3 %shard_map.68 = (f32[2,8]{1,0:T(2,128)}, f32[3,4,2,8]{3,2,1,0:T(2,128)}) custom-call(f32[5184]{0:T(1024)} %constant.2.clone.table, f32[3]{0:T(128)} %sub.1, s32[2,2,8]{2,1,0:T(2,128)} %off.1, f32[32,32,128]{2,1,0:T(8,128)} %img_hbm.1, f32[32,32,128]{2,1,0:T(8,128)} %fix_hbm.1), custom_call_target="tpu_custom_call" | custom-call | tf_op jit(solution)/shard_map/pallas_call | solution.py:579
  36.0 0.0 copy-start
  36.0 0.7 %copy-done = f32[2,8]{1,0:T(2,128)S(1)} copy-done((f32[2,8]{1,0:T(2,128)S(1)}, f32[2,8]{1,0:T(2,128)}, u32[]{:S(2)}) %copy-start) | copy-done | bytes 88
  36.6 0.6 %copy.9 = f32[2,8]{1,0:T(2,128)} copy(f32[2,8]{1,0:T(2,128)S(1)} %copy-done) | data formatting | bytes 128
  37.2 1.3 %copy.10 = f32[3,4,2,8]{3,2,1,0:T(2,128)} copy(f32[3,4,2,8]{3,2,1,0:T(2,128)} %get-tuple-element.5) | data formatting | bytes 1536
Async XLA Ops:
  36.0 0.7 %copy-start = (f32[2,8]{1,0:T(2,128)S(1)}, f32[2,8]{1,0:T(2,128)}, u32[]{:S(2)}) copy-start(f32[2,8]{1,0:T(2,128)} %get-tuple-element.4) | copy-start | bytes 196

commit v3 on v2

--- a/solution.py
+++ b/solution.py
@@ -101,10 +101,11 @@
 def kernel(
     cfg, table, sub, off, img_hbm, fix_hbm, ncc_out, grad_out,
     img, fix, in_sem, uz, zrecv, cz, ux, xl, xr, ce, packl, packr, yl, yr, ends3, w0, w1, g0, g1, hs,
-    ft, wv, px, py, pz, proj, stat, statr, part, gather,
+    ft, wv, px, py, pz, proj, stat, statr, part, out_tiles, gather,
     s_send, s_recv, f_send, f_recv,
 ):
     (nx_dev, ny_dev, width_t, nz, nx, ny, dz, dx, dy, zp, ex) = cfg
+    zu = -(-(dz + 3) // 4) * 4
     me_x, me_y, me_z = (lax.axis_index(a) for a in ("gx", "gy", "gz"))
     other_z = 1 - me_z
     start_x, start_y, start_z = me_x * dx, me_y * dy, me_z * dz
@@ -151,19 +152,16 @@
         return state + coef(0, 0, start_z + r) * img[r]
     lax.fori_loop(0, dz, zback, jnp.zeros((dx, dy), F32), unroll=True)
 
-    pl.semaphore_wait(barrier, count)
-    first = jnp.where(me_z == 0, dz - 2, 0)
-    z_copy = pltpu.make_async_remote_copy(
-        src_ref=uz.at[pl.ds(first, 2)], dst_ref=zrecv, send_sem=s_send.at[0], recv_sem=s_recv.at[0],
-        device_id=(me_x, me_y, other_z), device_id_type=MESH)
-    z_copy.start()
-
     has_l, has_r = me_x > 0, me_x < nx_dev - 1
     has_d, has_u = me_y > 0, me_y < ny_dev - 1
     for have, ref in ((has_l, xl), (has_r, xr), (has_d, yl), (has_u, yr)):
         @pl.when(jnp.logical_not(have))
         def _(ref=ref):
             ref[...] = jnp.zeros(ref.shape, F32)
+
+    if zu < zp:
+        xl[:, zu:] = jnp.zeros((HALO, zp - zu, dy), F32)
+        xr[:, zu:] = jnp.zeros((HALO, zp - zu, dy), F32)
 
     tz, sz = taps_of(sub[0])
     tx, sx = taps_of(sub[1])
@@ -251,6 +249,13 @@
         ft[BRICK * b:BRICK * b + BRICK] = cf
         sff.append(jnp.sum(jnp.sum(cf * cf, axis=0), axis=0, keepdims=True))
 
+    pl.semaphore_wait(barrier, count)
+    first = jnp.where(me_z == 0, dz - 2, 0)
+    z_copy = pltpu.make_async_remote_copy(
+        src_ref=uz.at[pl.ds(first, 2)], dst_ref=zrecv, send_sem=s_send.at[0], recv_sem=s_recv.at[0],
+        device_id=(me_x, me_y, other_z), device_id_type=MESH)
+    z_copy.start()
+
     z_copy.wait()
     left_on = jnp.where(me_z == 1, 1.0, 0.0)
     right_on = 1.0 - left_on
@@ -319,7 +324,7 @@
         ce[i] = jnp.zeros((zp, dy), F32)
     waits_x, waits_y = [], []
     for c in range(nch):
-        zs = pl.ds(8 * c, 8)
+        zs = pl.ds(8 * c, min(8, zu - 8 * c))
         waits_x.append(pair(
             ux.at[pl.ds(0, HALO), zs], xr.at[:, zs], ux.at[pl.ds(dx - HALO, HALO), zs], xl.at[:, zs],
             6 + 2 * c, (me_x - 1, me_y, me_z), (me_x + 1, me_y, me_z), has_l, has_r))
@@ -497,13 +502,18 @@
                 accs[b + e] = t if accs[b + e] is None else accs[b + e] + t
         for e in range(ne):
             for k in range(nk):
-                part[e, d * nk + k:d * nk + k + 1, :] = jnp.sum(accs[e] * bz[k], axis=0, keepdims=True)
-    for e in range(ne):
-        part[e, 3 * nk:] = jnp.zeros((part.shape[1] - 3 * nk, dy), F32)
-    depth = part.shape[1]
-    full = jnp.dot(part[...].reshape(ne * depth, dy), by_mat, precision=HIGHEST,
-                   preferred_element_type=F32) * (1.0 / SUPPORT_NORM)
-    part[...] = full.reshape(ne, depth, dy)
+                row = e * 3 * nk + d * nk + k
+                part[row:row + 1, :] = jnp.sum(accs[e] * bz[k], axis=0, keepdims=True)
+    full = jnp.dot(part[...], by_mat, precision=HIGHEST, preferred_element_type=F32) * (1.0 / SUPPORT_NORM)
+    tiles = nbx * 3 * nk // 8
+    for ix in range(3):
+        first_row = (0, 2, nbx + 2)[ix] * 3 * nk
+        tile = None
+        for g in range(tiles):
+            t = full[first_row + 8 * g:first_row + 8 * g + 8]
+            t = t if g == 0 else pltpu.roll(t, 16 * g, 1)
+            tile = t if tile is None else tile + t
+        out_tiles[ix] = tile
 
     def slot_of(ix, iy, iz):
         return ((ix + 1) * 3 + (iy + 1)) * 2 + iz
@@ -517,7 +527,7 @@
         @pl.when(ok)
         def _(ix=ix, there=there, target=target):
             pltpu.make_async_remote_copy(
-                src_ref=part.at[pl.ds(2 + nbx * ix if ix >= 0 else 0, nbx)],
+                src_ref=out_tiles.at[ix + 1],
                 dst_ref=gather.at[there], send_sem=f_send.at[there], recv_sem=f_recv.at[there],
                 device_id=target, device_id_type=MESH).start()
     for ix, iy, iz, ok, target in peers:
@@ -526,15 +536,15 @@
         @pl.when(ok)
         def _(ix=ix, there=there, here=here, target=target):
             pltpu.make_async_remote_copy(
-                src_ref=part.at[pl.ds(2 + nbx * ix if ix >= 0 else 0, nbx)],
+                src_ref=out_tiles.at[ix + 1],
                 dst_ref=gather.at[there], send_sem=f_send.at[there], recv_sem=f_recv.at[there],
                 device_id=target, device_id_type=MESH).wait_send()
             pltpu.make_async_remote_copy(
-                src_ref=part.at[pl.ds(0, nbx)],
+                src_ref=out_tiles.at[0],
                 dst_ref=gather.at[here], send_sem=f_send.at[here], recv_sem=f_recv.at[here],
                 device_id=target, device_id_type=MESH).wait_recv()
-    gather_own = part[2:2 + nbx]
-    lane_c = iota((nbx * depth, dy), 1)
+    gather_own = out_tiles[1]
+    lane_c = iota((8, dy), 1) & 15
     result = None
     for iy in (-1, 0, 1):
         total = gather_own if iy == 0 else None
@@ -544,7 +554,6 @@
                     continue
                 v = gather[slot_of(ix, iy, iz)]
                 total = v if total is None else total + v
-        total = total.reshape(nbx * depth, dy)
         if iy == 0:
             moved = pltpu.roll(total, dy - 2, 1)
         elif iy < 0:
@@ -552,11 +561,12 @@
         else:
             moved = jnp.where(lane_c >= nby - 2, pltpu.roll(total, nby - 2, 1), 0.0)
         result = moved if result is None else result + moved
-    for i in range(nbx):
-        for d in range(3):
-            for k in range(nk):
-                row = i * depth + d * nk + k
-                grad_out[d, k, i:i + 1, :] = result[row:row + 1, :nby]
+    for g in range(tiles):
+        t = result if g == 0 else pltpu.roll(result, dy - 16 * g, 1)
+        for q in range(8):
+            i, rest = divmod(8 * g + q, 3 * nk)
+            d, k = divmod(rest, nk)
+            grad_out[d, k, i:i + 1, :] = t[q:q + 1, :nby]
 
 
 def shards(sizes, moving_image, fixed_image, subvoxel, brick_offset):
@@ -570,7 +580,6 @@
     rows = ex // nslot
     nch = zp // 8
     nbx, nby, nk = dx // BRICK, dy // BRICK, nz // BRICK
-    depth = -(-3 * nk // 8) * 8
     cfg = (nx_dev, ny_dev, width_t, nz, nx, ny, dz, dx, dy, zp, ex)
     vm = lambda *shape: pltpu.VMEM(shape, F32)
     vspec = pl.BlockSpec(memory_space=pltpu.VMEM)
@@ -595,7 +604,7 @@
             vm(dx, dz, dy), vm(dx, dz, dy), vm(dx, dz, dy), vm(dx, dz, dy), vm(dx, dz, dy),
             vm(3 * nbx * 3 * 5, dz, dy),
             vm(2, 8, dy), vm(2, 8, dy),
-            vm(nbx + 4, depth, dy), vm(18, nbx, depth, dy),
+            vm((nbx + 4) * 3 * nk, dy), vm(3, 8, dy), vm(18, 8, dy),
             pltpu.SemaphoreType.DMA((6 + 4 * nch,)), pltpu.SemaphoreType.DMA((6 + 4 * nch,)),
             pltpu.SemaphoreType.DMA((18,)), pltpu.SemaphoreType.DMA((18,)),
         ],

time: 38.8 us -> 39.6 us (1.021)
  Pallas kernels: 35.3 us -> 36 us
    pallas_call x1, Pallas kernels: 35.3 us -> 36 us  [shards(): pl.pallas_call(functools.partial(kernel, cfg), out_shape=(jax.ShapeDtypeS...]
where the time goes in v3:
time: 39.6 us; the launch traced here: 39.2 us
  Pallas kernels  36 us (91%)
  local copies, waits for them, and re-layouts  2.53 us (6%)
  between operations  0.65 us (2%)
    pallas_call x1, Pallas kernels, shards(): pl.pallas_call(functools.partial(kernel, cfg), out_shape=(jax.ShapeDtypeS...  36 us
    unnamed x4, local copies, waits for them, and re-layouts  2.53 us

profile of v3, /device:TPU:1, one launch (start us, length us, event | category | flops | bytes accessed | tf_op | source)
XLA Modules:
  0.0 39.2 jit_solution(1121590019367152885)
XLA Ops:
  0.6 36.0 %shard_map.68 = (f32[2,8]{1,0:T(2,128)}, f32[3,4,2,8]{3,2,1,0:T(2,128)}) custom-call(f32[5184]{0:T(1024)} %constant.2.clone.table, f32[3]{0:T(128)} %sub.1, s32[2,2,8]{2,1,0:T(2,128)} %off.1, f32[32,32,128]{2,1,0:T(8,128)} %img_hbm.1, f32[32,32,128]{2,1,0:T(8,128)} %fix_hbm.1), custom_call_target="tpu_custom_call" | custom-call | tf_op jit(solution)/shard_map/pallas_call | solution.py:588
  36.7 0.0 copy-start
  36.7 0.7 %copy-done = f32[2,8]{1,0:T(2,128)S(1)} copy-done((f32[2,8]{1,0:T(2,128)S(1)}, f32[2,8]{1,0:T(2,128)}, u32[]{:S(2)}) %copy-start) | copy-done | bytes 88
  37.4 0.6 %copy.9 = f32[2,8]{1,0:T(2,128)} copy(f32[2,8]{1,0:T(2,128)S(1)} %copy-done) | data formatting | bytes 128
  37.9 1.3 %copy.10 = f32[3,4,2,8]{3,2,1,0:T(2,128)} copy(f32[3,4,2,8]{3,2,1,0:T(2,128)} %get-tuple-element.5) | data formatting | bytes 1536
Async XLA Ops:
  36.7 0.7 %copy-start = (f32[2,8]{1,0:T(2,128)S(1)}, f32[2,8]{1,0:T(2,128)}, u32[]{:S(2)}) copy-start(f32[2,8]{1,0:T(2,128)} %get-tuple-element.4) | copy-start | bytes 196

commit v4 on v3

--- a/solution.py
+++ b/solution.py
@@ -105,7 +105,6 @@
     s_send, s_recv, f_send, f_recv,
 ):
     (nx_dev, ny_dev, width_t, nz, nx, ny, dz, dx, dy, zp, ex) = cfg
-    zu = -(-(dz + 3) // 4) * 4
     me_x, me_y, me_z = (lax.axis_index(a) for a in ("gx", "gy", "gz"))
     other_z = 1 - me_z
     start_x, start_y, start_z = me_x * dx, me_y * dy, me_z * dz
@@ -152,6 +151,13 @@
         return state + coef(0, 0, start_z + r) * img[r]
     lax.fori_loop(0, dz, zback, jnp.zeros((dx, dy), F32), unroll=True)
 
+    pl.semaphore_wait(barrier, count)
+    first = jnp.where(me_z == 0, dz - 2, 0)
+    z_copy = pltpu.make_async_remote_copy(
+        src_ref=uz.at[pl.ds(first, 2)], dst_ref=zrecv, send_sem=s_send.at[0], recv_sem=s_recv.at[0],
+        device_id=(me_x, me_y, other_z), device_id_type=MESH)
+    z_copy.start()
+
     has_l, has_r = me_x > 0, me_x < nx_dev - 1
     has_d, has_u = me_y > 0, me_y < ny_dev - 1
     for have, ref in ((has_l, xl), (has_r, xr), (has_d, yl), (has_u, yr)):
@@ -159,9 +165,78 @@
         def _(ref=ref):
             ref[...] = jnp.zeros(ref.shape, F32)
 
-    if zu < zp:
-        xl[:, zu:] = jnp.zeros((HALO, zp - zu, dy), F32)
-        xr[:, zu:] = jnp.zeros((HALO, zp - zu, dy), F32)
+    z_copy.wait()
+    left_on = jnp.where(me_z == 1, 1.0, 0.0)
+    right_on = 1.0 - left_on
+    zl = zrecv[1] * left_on
+    zr0, zr1 = zrecv[0] * right_on, zrecv[1] * right_on
+    def zf(i, y):
+        y = coef(0, 1, start_z + i) * y
+        cz[i + 1] = uz[i] + y
+        return y
+    lax.fori_loop(0, dz, zf, zl, unroll=True)
+    y = coef(0, 1, start_z + dz) * cz[dz]
+    cz[dz + 1] = zr0 + y
+    y = coef(0, 1, start_z + dz + 1) * y
+    cz[dz + 2] = zr1 + y
+    def zb(i, y):
+        r = dz - 1 - i
+        y = coef(0, 2, start_z + r) * y
+        cz[r + 1] = cz[r + 1] + y
+        return y
+    y = lax.fori_loop(0, dz, zb, zr0, unroll=True)
+    cz[0] = zl + coef(0, 2, start_z - 1) * (uz[0] + y)
+    for i in range(dz + 3, zp):
+        cz[i] = jnp.zeros((dx, dy), F32)
+    for i in range(dx // 8):
+        ce[HALO - 1 + 8 * i:HALO - 1 + 8 * i + 8] = jnp.swapaxes(cz[:, 8 * i:8 * i + 8, :], 0, 1)
+
+    def xf(i, y):
+        y = coef(1, 0, start_x + i) * ce[HALO - 1 + i] + coef(1, 1, start_x + i) * y
+        ux[i] = y
+        return y
+    lax.fori_loop(0, dx, xf, jnp.zeros((zp, dy), F32), unroll=True)
+    def xb(i, y):
+        r = dx - 1 - i
+        y = coef(1, 2, start_x + r) * y
+        ux[r] = ux[r] + y
+        return y + coef(1, 0, start_x + r) * ce[HALO - 1 + r]
+    lax.fori_loop(0, dx, xb, jnp.zeros((zp, dy), F32), unroll=True)
+
+    def pair(low_src, low_dst, high_src, high_dst, sem, low_id, high_id, low_ok, high_ok):
+        low = pltpu.make_async_remote_copy(
+            src_ref=low_src, dst_ref=low_dst, send_sem=s_send.at[sem], recv_sem=s_recv.at[sem],
+            device_id=low_id, device_id_type=MESH)
+        high = pltpu.make_async_remote_copy(
+            src_ref=high_src, dst_ref=high_dst, send_sem=s_send.at[sem + 1], recv_sem=s_recv.at[sem + 1],
+            device_id=high_id, device_id_type=MESH)
+        @pl.when(low_ok)
+        def _():
+            low.start()
+        @pl.when(high_ok)
+        def _():
+            high.start()
+        def wait():
+            @pl.when(low_ok)
+            def _():
+                low.wait_send()
+                high.wait_recv()
+            @pl.when(high_ok)
+            def _():
+                high.wait_send()
+                low.wait_recv()
+        return wait
+
+    nch, nslot = zp // 8, dy // HALO
+    rows = ex // nslot
+    for i in range(dx + 2 * HALO - 1, ex):
+        ce[i] = jnp.zeros((zp, dy), F32)
+    waits_x, waits_y = [], []
+    for c in range(nch):
+        zs = pl.ds(8 * c, 8)
+        waits_x.append(pair(
+            ux.at[pl.ds(0, HALO), zs], xr.at[:, zs], ux.at[pl.ds(dx - HALO, HALO), zs], xl.at[:, zs],
+            6 + 2 * c, (me_x - 1, me_y, me_z), (me_x + 1, me_y, me_z), has_l, has_r))
 
     tz, sz = taps_of(sub[0])
     tx, sx = taps_of(sub[1])
@@ -248,86 +323,6 @@
         cf = ft[BRICK * b:BRICK * b + BRICK] - mean_f[b:b + 1][None]
         ft[BRICK * b:BRICK * b + BRICK] = cf
         sff.append(jnp.sum(jnp.sum(cf * cf, axis=0), axis=0, keepdims=True))
-
-    pl.semaphore_wait(barrier, count)
-    first = jnp.where(me_z == 0, dz - 2, 0)
-    z_copy = pltpu.make_async_remote_copy(
-        src_ref=uz.at[pl.ds(first, 2)], dst_ref=zrecv, send_sem=s_send.at[0], recv_sem=s_recv.at[0],
-        device_id=(me_x, me_y, other_z), device_id_type=MESH)
-    z_copy.start()
-
-    z_copy.wait()
-    left_on = jnp.where(me_z == 1, 1.0, 0.0)
-    right_on = 1.0 - left_on
-    zl = zrecv[1] * left_on
-    zr0, zr1 = zrecv[0] * right_on, zrecv[1] * right_on
-    def zf(i, y):
-        y = coef(0, 1, start_z + i) * y
-        cz[i + 1] = uz[i] + y
-        return y
-    lax.fori_loop(0, dz, zf, zl, unroll=True)
-    y = coef(0, 1, start_z + dz) * cz[dz]
-    cz[dz + 1] = zr0 + y
-    y = coef(0, 1, start_z + dz + 1) * y
-    cz[dz + 2] = zr1 + y
-    def zb(i, y):
-        r = dz - 1 - i
-        y = coef(0, 2, start_z + r) * y
-        cz[r + 1] = cz[r + 1] + y
-        return y
-    y = lax.fori_loop(0, dz, zb, zr0, unroll=True)
-    cz[0] = zl + coef(0, 2, start_z - 1) * (uz[0] + y)
-    for i in range(dz + 3, zp):
-        cz[i] = jnp.zeros((dx, dy), F32)
-    for i in range(dx // 8):
-        ce[HALO - 1 + 8 * i:HALO - 1 + 8 * i + 8] = jnp.swapaxes(cz[:, 8 * i:8 * i + 8, :], 0, 1)
-
-    def xf(i, y):
-        y = coef(1, 0, start_x + i) * ce[HALO - 1 + i] + coef(1, 1, start_x + i) * y
-        ux[i] = y
-        return y
-    lax.fori_loop(0, dx, xf, jnp.zeros((zp, dy), F32), unroll=True)
-    def xb(i, y):
-        r = dx - 1 - i
-        y = coef(1, 2, start_x + r) * y
-        ux[r] = ux[r] + y
-        return y + coef(1, 0, start_x + r) * ce[HALO - 1 + r]
-    lax.fori_loop(0, dx, xb, jnp.zeros((zp, dy), F32), unroll=True)
-
-    def pair(low_src, low_dst, high_src, high_dst, sem, low_id, high_id, low_ok, high_ok):
-        low = pltpu.make_async_remote_copy(
-            src_ref=low_src, dst_ref=low_dst, send_sem=s_send.at[sem], recv_sem=s_recv.at[sem],
-            device_id=low_id, device_id_type=MESH)
-        high = pltpu.make_async_remote_copy(
-            src_ref=high_src, dst_ref=high_dst, send_sem=s_send.at[sem + 1], recv_sem=s_recv.at[sem + 1],
-            device_id=high_id, device_id_type=MESH)
-        @pl.when(low_ok)
-        def _():
-            low.start()
-        @pl.when(high_ok)
-        def _():
-            high.start()
-        def wait():
-            @pl.when(low_ok)
-            def _():
-                low.wait_send()
-                high.wait_recv()
-            @pl.when(high_ok)
-            def _():
-                high.wait_send()
-                low.wait_recv()
-        return wait
-
-    nch = zp // 8
-    rows = ex // nslot
-    for i in range(dx + 2 * HALO - 1, ex):
-        ce[i] = jnp.zeros((zp, dy), F32)
-    waits_x, waits_y = [], []
-    for c in range(nch):
-        zs = pl.ds(8 * c, min(8, zu - 8 * c))
-        waits_x.append(pair(
-            ux.at[pl.ds(0, HALO), zs], xr.at[:, zs], ux.at[pl.ds(dx - HALO, HALO), zs], xl.at[:, zs],
-            6 + 2 * c, (me_x - 1, me_y, me_z), (me_x + 1, me_y, me_z), has_l, has_r))
 
     def combine(c):
         zs = pl.ds(8 * c, 8)

time: 39.6 us -> 38.7 us (0.977)
  Pallas kernels: 36 us -> 35.2 us
    pallas_call x1, Pallas kernels: 36 us -> 35.2 us  [shards(): pl.pallas_call(functools.partial(kernel, cfg), out_shape=(jax.ShapeDtypeS...]
where the time goes in v4:
time: 38.7 us; the launch traced here: 38.4 us
  Pallas kernels  35.2 us (91%)
  local copies, waits for them, and re-layouts  2.53 us (7%)
  between operations  0.65 us (2%)
    pallas_call x1, Pallas kernels, shards(): pl.pallas_call(functools.partial(kernel, cfg), out_shape=(jax.ShapeDtypeS...  35.2 us
    unnamed x4, local copies, waits for them, and re-layouts  2.53 us

profile of v4, /device:TPU:1, one launch (start us, length us, event | category | flops | bytes accessed | tf_op | source)
XLA Modules:
  0.0 38.4 jit_solution(11047628439526444464)
XLA Ops:
  0.6 35.2 %shard_map.68 = (f32[2,8]{1,0:T(2,128)}, f32[3,4,2,8]{3,2,1,0:T(2,128)}) custom-call(f32[5184]{0:T(1024)} %constant.2.clone.table, f32[3]{0:T(128)} %sub.1, s32[2,2,8]{2,1,0:T(2,128)} %off.1, f32[32,32,128]{2,1,0:T(8,128)} %img_hbm.1, f32[32,32,128]{2,1,0:T(8,128)} %fix_hbm.1), custom_call_target="tpu_custom_call" | custom-call | tf_op jit(solution)/shard_map/pallas_call | solution.py:583
  35.9 0.0 copy-start
  35.9 0.7 %copy-done = f32[2,8]{1,0:T(2,128)S(1)} copy-done((f32[2,8]{1,0:T(2,128)S(1)}, f32[2,8]{1,0:T(2,128)}, u32[]{:S(2)}) %copy-start) | copy-done | bytes 88
  36.5 0.6 %copy.9 = f32[2,8]{1,0:T(2,128)} copy(f32[2,8]{1,0:T(2,128)S(1)} %copy-done) | data formatting | bytes 128
  37.1 1.3 %copy.10 = f32[3,4,2,8]{3,2,1,0:T(2,128)} copy(f32[3,4,2,8]{3,2,1,0:T(2,128)} %get-tuple-element.5) | data formatting | bytes 1536
Async XLA Ops:
  35.9 0.7 %copy-start = (f32[2,8]{1,0:T(2,128)S(1)}, f32[2,8]{1,0:T(2,128)}, u32[]{:S(2)}) copy-start(f32[2,8]{1,0:T(2,128)} %get-tuple-element.4) | copy-start | bytes 196
